TPU v7x, 32 devices: a whole 2x2x4 slice. The times are simulated.
32 devices in a mesh: year: 4 (over z), row: 2 (over x), col: 4 (over y, core).
Axes of the slice: x: 2, y: 2, z: 4, core: 2. Of those that a mesh axis runs over, the one named last changes fastest.
Arguments:
- observed: float32 [4, 46, 128, 512], P('year', None, 'row', 'col'), may hold values from 0 to 0.8
- quality: int32 [4, 46, 128, 512], P('year', None, 'row', 'col'), may hold values from 0 to 3, as said below
- land_mask: int32 [128, 512], P('row', 'col'), may hold values 0 or 1
- params: float32 [4, 7, 128, 512], P('year', None, 'row', 'col'), may hold values from -0.3 to 3.4
- spatial_weight: float32 [7], replicated, may hold values from 0.2 to 2
- temporal_weight: float32 [7], replicated, may hold values from 0.2 to 2
Outputs:
- new_params: float32 [4, 7, 128, 512], P('year', None, 'row', 'col')
- residual: float32 [4, 7, 128, 512], P('year', None, 'row', 'col')
Inputs may be any that keep to these rules, and one draw needn't show every extreme that they name: `quality`: 0 good, 1 marginal, 2 snow, 3 cloud.
All inputs are finite; a program needn't handle non-finite values. No bound on the sum of `land_mask` on one device may be relied on, other than what follows from the above.
Results may differ from a plain program's by a relative error of at most 0.0003.
Values sent between devices are 32-bit elements; how exact they have to be, the bound alone decides.
A program may use at most 64 MiB of HBM per device.

v0:
```python
import functools

import jax
import jax.numpy as jnp
from jax import lax
from jax.experimental import pallas as pl
from jax.experimental.pallas import tpu as pltpu
from jax.sharding import PartitionSpec as P

ITERS = 4
ROUNDS = ITERS + 1
SUB = 8
BLOCKS = 2
DAMPING = 0.1
MESH = pl.DeviceIdType.MESH


def pairs_of(count):
    return [(i, j) for i in range(count) for j in range(i, count)]


def kernel(
    sizes,
    observed,
    quality,
    land,
    params,
    spatial,
    temporal,
    new_params,
    residual,
    obs,
    qual,
    field,
    inverse,
    resid,
    moments,
    slots,
    load_sem,
    send_sem,
    recv_sem,
    row_send,
    row_recv,
    sum_send,
    sum_recv,
):
    n_year, n_row, n_col = sizes
    dates, rows, cols = obs.shape
    count = resid.shape[1]
    step_rows = SUB * BLOCKS
    chunks = rows // step_rows
    pairs = pairs_of(count)
    place = {pair: at for at, pair in enumerate(pairs)}

    year, row, col = lax.axis_index("year"), lax.axis_index("row"), lax.axis_index("col")
    even = lax.rem(row, 2) == 0

    has_prev, has_next = year > 0, year < n_year - 1
    has_left, has_right = col > 0, col < n_col - 1
    has_up, has_down = row > 0, row < n_row - 1
    has_first = jnp.logical_or(jnp.logical_and(even, has_up), jnp.logical_and(~even, has_down))
    has_last = jnp.logical_or(jnp.logical_and(even, has_down), jnp.logical_and(~even, has_up))
    toward_first = row + jnp.where(even, -1, 1)
    toward_last = row + jnp.where(even, 1, -1)

    def chunk_rows(position):
        chunk = jnp.where(even, position, chunks - 1 - position)
        return pl.multiple_of(chunk * step_rows, step_rows)

    param_load = pltpu.make_async_copy(
        params.at[0], field.at[0, 0, :, pl.ds(SUB, rows), :], load_sem.at[0]
    )
    param_load.start()

    def input_loads(position):
        start = chunk_rows(position)
        where = (slice(None), pl.ds(start, step_rows), slice(None))
        return (
            pltpu.make_async_copy(observed.at[0].at[where], obs.at[where], load_sem.at[1 + 2 * position]),
            pltpu.make_async_copy(quality.at[0].at[where], qual.at[where], load_sem.at[2 + 2 * position]),
        )

    for position in range(chunks):
        for copy in input_loads(position):
            copy.start()

    total_devices = n_year * n_row * n_col
    near = (n_year - 1) + (n_row - 1) <= ITERS

    def peer(other):
        spot = lax.rem((year * n_row + row) * n_col + col + other, total_devices)
        return (spot // (n_row * n_col), lax.rem(spot // n_col, n_row), lax.rem(spot, n_col))

    barrier = pltpu.get_barrier_semaphore()
    if near:
        for other in range(1, n_col):
            pl.semaphore_signal(
                barrier,
                inc=1,
                device_id=(year, row, lax.rem(col + other, n_col)),
                device_id_type=MESH,
            )
        expected = n_col - 1
        for present, target in (
            (has_prev, (year - 1, row, col)),
            (has_next, (year + 1, row, col)),
            (has_up, (year, row - 1, col)),
            (has_down, (year, row + 1, col)),
        ):
            @pl.when(present)
            def _(target=target):
                pl.semaphore_signal(barrier, inc=1, device_id=target, device_id_type=MESH)

            expected = expected + present.astype(jnp.int32)
        pl.semaphore_wait(barrier, expected)
    else:
        for other in range(1, total_devices):
            pl.semaphore_signal(barrier, inc=1, device_id=peer(other), device_id_type=MESH)
        pl.semaphore_wait(barrier, total_devices - 1)

    sides = (
        (has_next, (year + 1, row, col), 1, has_prev),
        (has_prev, (year - 1, row, col), 2, has_next),
        (has_right, (year, row, col + 1), 3, has_left),
        (has_left, (year, row, col - 1), 4, has_right),
    )

    def side_copy(step, position, side):
        _, target, slot, _ = sides[side]
        where = pl.ds(chunk_rows(position) + SUB, step_rows)
        return pltpu.make_async_remote_copy(
            src_ref=field.at[step, 0, :, where, :],
            dst_ref=field.at[step, slot, :, where, :],
            send_sem=send_sem.at[step, side, position],
            recv_sem=recv_sem.at[step, side, position],
            device_id=target,
            device_id_type=MESH,
        )

    def row_copy(step, last):
        top = jnp.logical_xor(even, last)
        source = pl.multiple_of(jnp.where(top, SUB, rows), SUB)
        target = pl.multiple_of(jnp.where(top, rows + SUB, 0), SUB)
        return pltpu.make_async_remote_copy(
            src_ref=field.at[step, 0, :, pl.ds(source, SUB), :],
            dst_ref=field.at[step, 0, :, pl.ds(target, SUB), :],
            send_sem=row_send.at[step, int(last)],
            recv_sem=row_recv.at[step, int(last)],
            device_id=(year, toward_last if last else toward_first, col),
            device_id_type=MESH,
        )

    def start_sends(step, position):
        for side in range(4):
            @pl.when(sides[side][0])
            def _(side=side):
                side_copy(step, position, side).start()

    def wait_sides(step, position):
        for side in range(4):
            @pl.when(sides[side][3])
            def _(side=side):
                side_copy(step, position, side).wait_recv()

    def close_edges(step, first, last):
        for flag, at_last, present in ((first, False, has_first), (last, True, has_last)):
            top = jnp.logical_xor(even, at_last)

            @pl.when(jnp.logical_and(flag, present))
            def _(at_last=at_last):
                row_copy(step, at_last).start()

            def repeat(source, edge, target):
                for p in range(count):
                    block = field[step, 0, p, source : source + SUB, :]
                    field[step, 0, p, target : target + SUB, :] = jnp.broadcast_to(
                        block[edge : edge + 1, :], (SUB, cols)
                    )

            @pl.when(jnp.logical_and(jnp.logical_and(flag, ~present), top))
            def _():
                repeat(SUB, 0, 0)

            @pl.when(jnp.logical_and(jnp.logical_and(flag, ~present), ~top))
            def _():
                repeat(rows, SUB - 1, rows + SUB)

    def wait_edges(step, first, last):
        for flag, at_last, present in ((first, False, has_first), (last, True, has_last)):
            @pl.when(jnp.logical_and(flag, present))
            def _(at_last=at_last):
                row_copy(step, at_last).wait_recv()

    param_load.wait()

    def send_params(position, carry):
        start_sends(0, position)
        return carry

    lax.fori_loop(0, chunks, send_params, 0)
    close_edges(0, True, True)

    prev_slot = jnp.where(has_prev, 1, 0)
    next_slot = jnp.where(has_next, 2, 0)
    left_slot = jnp.where(has_left, 3, 0)
    right_slot = jnp.where(has_right, 4, 0)
    lane = lax.broadcasted_iota(jnp.int32, (SUB, cols), 1)
    level = lax.broadcasted_iota(jnp.int32, (SUB, cols), 0)
    lane_first, lane_last = lane == 0, lane == cols - 1
    level_first, level_last = level == 0, level == SUB - 1
    grid_left = lane == jnp.where(has_left, -1, 0)
    grid_right = lane == jnp.where(has_right, -1, cols - 1)

    def around(step, p, start):
        own = pl.ds(start + SUB, SUB)
        here = field[step, 0, p, own, :]
        above = field[step, 0, p, pl.ds(start, SUB), :]
        below = field[step, 0, p, pl.ds(start + 2 * SUB, SUB), :]
        up = pltpu.roll(jnp.where(level_last, above, here), 1, 0)
        down = pltpu.roll(jnp.where(level_first, below, here), SUB - 1, 0)
        left = pltpu.roll(jnp.where(lane_last, field[step, left_slot, p, own, :], here), 1, 1)
        right = pltpu.roll(
            jnp.where(lane_first, field[step, right_slot, p, own, :], here), cols - 1, 1
        )
        left = jnp.where(grid_left, here, left)
        right = jnp.where(grid_right, here, right)
        plane = (up + down) + (left + right)
        yearly = field[step, prev_slot, p, own, :] + field[step, next_slot, p, own, :]
        return here, spatial[p] * plane + temporal[p] * yearly

    def precondition(start, values):
        rows_here = pl.ds(start, SUB)
        entry = [inverse[at, rows_here, :] for at in range(len(pairs))]
        outs = []
        for p in range(count):
            total = entry[place[(0, p)]] * values[0]
            for q in range(1, count):
                total = total + entry[place[(min(p, q), max(p, q))]] * values[q]
            outs.append(total)
        return outs

    def dot(left, right):
        terms = [a * b for a, b in zip(left, right)]
        while len(terms) > 1:
            terms = [sum(terms[i : i + 2][1:], terms[i]) for i in range(0, len(terms), 2)]
        return terms[0]

    def normal(start):
        here = pl.ds(start, SUB)
        base, peak, slope, rise_mid, rise_log, fall_mid, fall_log = [
            field[0, 0, p, pl.ds(start + SUB, SUB), :] for p in range(count)
        ]
        rise_rate, fall_rate = jnp.exp(rise_log), jnp.exp(fall_log)
        rise_half, fall_half = 0.5 * rise_rate, 0.5 * fall_rate

        def date_step(date, sums):
            time = date.astype(jnp.float32) * (1.0 / dates)
            flag = qual[date, here, :].astype(jnp.float32)
            weight = jnp.maximum(1.0 - 0.5 * flag, 0.0)
            rise_gap = time - rise_mid
            fall_gap = time - fall_mid
            rise = jnp.tanh(rise_half * rise_gap)
            fall = jnp.tanh(fall_half * fall_gap)
            season = rise - fall
            height = peak - slope * time
            rise_bell = height - height * (rise * rise)
            fall_bell = height - height * (fall * fall)
            basis = [
                None,
                season,
                time * season,
                rise_bell,
                rise_gap * rise_bell,
                fall_bell,
                fall_gap * fall_bell,
            ]
            weighted = [weight] + [weight * item for item in basis[1:]]
            out = []
            for i, j in pairs:
                term = weighted[j] if i == 0 else basis[i] * weighted[j]
                out.append(sums[place[(i, j)]] + term)
            seen = obs[date, here, :]
            for i in range(count):
                out.append(sums[len(pairs) + i] + seen * weighted[i])
            return tuple(out)

        zero = jnp.zeros((SUB, cols), jnp.float32)
        sums = lax.fori_loop(
            0, dates, date_step, (zero,) * (len(pairs) + count), unroll=dates
        )
        share = land[here, :].astype(jnp.float32) * (1.0 / dates)
        rise_scale, fall_scale = 0.25 * rise_rate, 0.25 * fall_rate
        scale = [None, 0.5, -0.5, -rise_scale, rise_scale, fall_scale, -fall_scale]
        shared = [share] + [share * item for item in scale[1:]]
        block = {}
        for i, j in pairs:
            factor = shared[j] if i == 0 else shared[j] * scale[i]
            block[(i, j)] = sums[place[(i, j)]] * factor
        for p in range(count):
            total = shared[p] * sums[len(pairs) + p]
            for q, value in ((0, base), (1, peak), (2, slope)):
                total = total - block[(min(p, q), max(p, q))] * value
            resid[0, p, here, :] = total
        for p in range(count):
            block[(p, p)] = block[(p, p)] + (DAMPING + 4.0 * spatial[p] + 2.0 * temporal[p])
        for k in range(count):
            turn = 1.0 / block[(k, k)]
            edge = {i: block[(min(i, k), max(i, k))] for i in range(count) if i != k}
            lean = {i: edge[i] * turn for i in edge}
            for i, j in pairs:
                if i != k and j != k:
                    block[(i, j)] = block[(i, j)] - edge[i] * lean[j]
            for i in edge:
                block[(min(i, k), max(i, k))] = lean[i]
            block[(k, k)] = -turn
        for pair in pairs:
            inverse[place[pair], here, :] = -block[pair]

    zero = jnp.zeros((SUB, cols), jnp.float32)

    def make_stage(stage):
        def body(position, carry):
            odd_sum, even_sum = carry
            start = chunk_rows(position)
            first, last = position == 0, position == chunks - 1
            if stage == 0:
                for copy in input_loads(position):
                    copy.wait()

                def each(b, c):
                    normal(pl.multiple_of(start + b * SUB, SUB))
                    return c

                lax.fori_loop(0, BLOCKS, each, 0)
            before = stage
            wait_sides(before, position)
            wait_edges(before, first, last)
            for b in range(BLOCKS):
                at = pl.multiple_of(start + b * SUB, SUB)
                rows_here = pl.ds(at, SUB)
                held, pushed = [], []
                for p in range(count):
                    here, push = around(before, p, at)
                    if stage == 0:
                        push = (resid[0, p, rows_here, :] + push) - (
                            4.0 * spatial[p] + 2.0 * temporal[p]
                        ) * here
                    resid[stage, p, rows_here, :] = push
                    held.append(here)
                    pushed.append(push)
                if stage > 0:
                    odd_sum = odd_sum + dot(held, pushed)
                if stage < ITERS:
                    turned = precondition(at, pushed)
                    for p in range(count):
                        field[stage + 1, 0, p, pl.ds(at + SUB, SUB), :] = turned[p]
                    even_sum = even_sum + dot(turned, pushed)
            if stage < ITERS:
                start_sends(stage + 1, position)
                close_edges(stage + 1, first, last)
            return odd_sum, even_sum

        return body

    sums = []
    for stage in range(ITERS + 1):
        odd_sum, even_sum = lax.fori_loop(0, chunks, make_stage(stage), (zero, zero))
        if stage > 0:
            sums.append(odd_sum)
        if stage < ITERS:
            sums.append(even_sum)

    for at, value in enumerate(sums):
        moments[at : at + 1, :] = jnp.sum(value, axis=0, keepdims=True)

    def sum_copy(other):
        return pltpu.make_async_remote_copy(
            src_ref=moments,
            dst_ref=slots.at[other - 1],
            send_sem=sum_send.at[other - 1],
            recv_sem=sum_recv.at[other - 1],
            device_id=peer(other),
            device_id_type=MESH,
        )

    for other in range(1, total_devices):
        sum_copy(other).start()
    for step in range(ROUNDS):
        def drain(position, carry, step=step):
            for side in range(4):
                @pl.when(sides[side][0])
                def _(side=side):
                    side_copy(step, position, side).wait_send()
            return carry

        lax.fori_loop(0, chunks, drain, 0)
        for at_last, present in ((False, has_first), (True, has_last)):
            @pl.when(present)
            def _(at_last=at_last, step=step):
                row_copy(step, at_last).wait_send()
    parts = [moments[...]]
    for other in range(1, total_devices):
        sum_copy(other).wait_recv()
        parts.append(slots[other - 1])
    while len(parts) > 1:
        parts = [sum(parts[i : i + 2][1:], parts[i]) for i in range(0, len(parts), 2)]
    total = parts[0]
    total = jnp.broadcast_to(jnp.sum(total, axis=1, keepdims=True), total.shape)
    mu = [total[at : at + 1, :] for at in range(2 * ITERS)]
    drop = [mu[at] - mu[at + 1] for at in range(2 * ITERS - 1)]

    def form(coefs, table):
        total = None
        for i, left in enumerate(coefs):
            for j in range(i, len(coefs)):
                term = left * coefs[j] * table[i + j]
                term = term if i == j else 2.0 * term
                total = term if total is None else total + term
        return total

    one = jnp.ones_like(mu[0])
    search, direction = [one], [one]
    lengths = [jnp.zeros_like(one)] * ITERS
    inner = mu[0]
    for sweep in range(ITERS):
        alpha = inner / form(direction, drop)
        for j in range(sweep + 1):
            lengths[j] = lengths[j] + alpha * direction[j]
        if sweep + 1 < ITERS:
            grown = []
            for j in range(sweep + 2):
                change = None
                if j <= sweep:
                    change = direction[j]
                if j > 0:
                    change = -direction[j - 1] if change is None else change - direction[j - 1]
                base = search[j] if j <= sweep else None
                grown.append(-alpha * change if base is None else base - alpha * change)
            search = grown
            fresh = form(search, mu)
            ratio = fresh / inner
            inner = fresh
            direction = [
                search[j] + ratio * direction[j] if j <= sweep else search[j]
                for j in range(sweep + 2)
            ]

    steps = [jnp.broadcast_to(value, (SUB, cols)) for value in lengths]
    mixes = [1.0 - steps[0]]
    mixes += [steps[j - 1] - steps[j] for j in range(1, ITERS)]
    mixes += [steps[-1]]

    def finish(b, carry):
        at = pl.multiple_of(b * SUB, SUB)
        rows_here = pl.ds(at, SUB)
        padded = pl.ds(at + SUB, SUB)
        for p in range(count):
            total = field[0, 0, p, padded, :]
            for j in range(ITERS):
                total = total + steps[j] * field[j + 1, 0, p, padded, :]
            new_params[0, p, rows_here, :] = total
            total = mixes[0] * resid[0, p, rows_here, :]
            for j in range(1, ITERS + 1):
                total = total + mixes[j] * resid[j, p, rows_here, :]
            residual[0, p, rows_here, :] = total
        return carry

    lax.fori_loop(0, rows // SUB, finish, 0)

    for other in range(1, total_devices):
        sum_copy(other).wait_send()


def per_device(sizes, observed, quality, land_mask, params, spatial_weight, temporal_weight):
    n_year, n_row, n_col = sizes
    _, dates, rows, cols = observed.shape
    count = params.shape[1]
    chunks = rows // (SUB * BLOCKS)
    others = n_year * n_row * n_col - 1
    f32 = jnp.float32
    vmem = pl.BlockSpec(memory_space=pltpu.VMEM)
    hbm = pl.BlockSpec(memory_space=pltpu.HBM)
    smem = pl.BlockSpec(memory_space=pltpu.SMEM)
    dma = pltpu.SemaphoreType.DMA
    return pl.pallas_call(
        functools.partial(kernel, sizes),
        out_shape=(
            jax.ShapeDtypeStruct(params.shape, f32),
            jax.ShapeDtypeStruct(params.shape, f32),
        ),
        in_specs=[hbm, hbm, vmem, hbm, smem, smem],
        out_specs=(vmem, vmem),
        scratch_shapes=[
            pltpu.VMEM((dates, rows, cols), f32),
            pltpu.VMEM((dates, rows, cols), jnp.int32),
            pltpu.VMEM((ROUNDS, 5, count, rows + 2 * SUB, cols), f32),
            pltpu.VMEM((count * (count + 1) // 2, rows, cols), f32),
            pltpu.VMEM((ROUNDS, count, rows, cols), f32),
            pltpu.VMEM((2 * ITERS, cols), f32),
            pltpu.VMEM((max(others, 1), 2 * ITERS, cols), f32),
            dma((1 + 2 * chunks,)),
            dma((ROUNDS, 4, chunks)),
            dma((ROUNDS, 4, chunks)),
            dma((ROUNDS, 2)),
            dma((ROUNDS, 2)),
            dma((max(others, 1),)),
            dma((max(others, 1),)),
        ],
        compiler_params=pltpu.CompilerParams(
            collective_id=0, has_side_effects=True, vmem_limit_bytes=67043328
        ),
        name="gauss_newton",
    )(observed, quality, land_mask, params, spatial_weight, temporal_weight)


def solution(mesh):
    sizes = tuple(mesh.shape[axis] for axis in ("year", "row", "col"))
    grid = P("year", None, "row", "col")
    return jax.shard_map(
        functools.partial(per_device, sizes),
        mesh=mesh,
        in_specs=(grid, grid, P("row", "col"), grid, P(), P()),
        out_specs=(grid, grid),
        check_vma=False,
    )
```

profile of v0, /device:TPU:0, one launch (start us, length us, event | category | flops | bytes accessed | tf_op | source)
XLA Modules:
  0.0 44.3 jit_solution(15578810598347944270)
XLA Ops:
  0.6 40.4 %gauss_newton.1 = (f32[1,7,64,128]{3,2,1,0:T(8,128)}, f32[1,7,64,128]{3,2,1,0:T(8,128)}) custom-call(f32[1,46,64,128]{3,2,1,0:T(8,128)} %observed.1, s32[1,46,64,128]{3,2,1,0:T(8,128)} %quality.1, s32[64,128]{1,0:T(8,128)} %land.1, f32[1,7,64,128]{3,2,1,0:T(8,128)} %params.1, f32[7]{0:T(128)} %spatial.1, f32[7]{0:T(128)} %temporal.1), custom_call_target="tpu_custom_call" | custom-call | tf_op jit(solution)/shard_map/gauss_newton/pallas_call | solution.py:485
  41.0 1.6 %copy.10 = f32[1,7,64,128]{3,2,1,0:T(8,128)} copy(f32[1,7,64,128]{3,2,1,0:T(8,128)} %get-tuple-element.4) | data formatting | bytes 458752
  42.7 1.6 %copy.11 = f32[1,7,64,128]{3,2,1,0:T(8,128)} copy(f32[1,7,64,128]{3,2,1,0:T(8,128)} %get-tuple-element.5) | data formatting | bytes 458752
where the time goes:
time: 44.5 us; the launch traced here: 44.3 us
  Pallas kernels  40.4 us (91%)
  local copies, waits for them, and re-layouts  3.28 us (7%)
  between operations  0.64 us (1%)
    pallas_call x1, Pallas kernels, per_device(): pl.pallas_call(functools.partial(kernel, sizes), out_shape=(jax.ShapeDtyp...  40.4 us
    unnamed x2, local copies, waits for them, and re-layouts  3.28 us

commit v1 on v0

--- a/solution.py
+++ b/solution.py
@@ -10,7 +10,8 @@
 ITERS = 4
 ROUNDS = ITERS + 1
 SUB = 8
-BLOCKS = 2
+BLOCKS = 1
+LEAD = 2
 DAMPING = 0.1
 MESH = pl.DeviceIdType.MESH
 
@@ -23,18 +24,23 @@
     sizes,
     observed,
     quality,
-    land,
+    land_mask,
     params,
-    spatial,
-    temporal,
+    spatial_weight,
+    temporal_weight,
     new_params,
     residual,
     obs,
     qual,
+    land,
+    spatial,
+    temporal,
     field,
     inverse,
     resid,
+    slope,
     moments,
+    notes,
     slots,
     load_sem,
     send_sem,
@@ -53,7 +59,7 @@
     place = {pair: at for at, pair in enumerate(pairs)}
 
     year, row, col = lax.axis_index("year"), lax.axis_index("row"), lax.axis_index("col")
-    even = lax.rem(row, 2) == 0
+    even = lax.rem(row, 2) == 1
 
     has_prev, has_next = year > 0, year < n_year - 1
     has_left, has_right = col > 0, col < n_col - 1
@@ -67,23 +73,6 @@
         chunk = jnp.where(even, position, chunks - 1 - position)
         return pl.multiple_of(chunk * step_rows, step_rows)
 
-    param_load = pltpu.make_async_copy(
-        params.at[0], field.at[0, 0, :, pl.ds(SUB, rows), :], load_sem.at[0]
-    )
-    param_load.start()
-
-    def input_loads(position):
-        start = chunk_rows(position)
-        where = (slice(None), pl.ds(start, step_rows), slice(None))
-        return (
-            pltpu.make_async_copy(observed.at[0].at[where], obs.at[where], load_sem.at[1 + 2 * position]),
-            pltpu.make_async_copy(quality.at[0].at[where], qual.at[where], load_sem.at[2 + 2 * position]),
-        )
-
-    for position in range(chunks):
-        for copy in input_loads(position):
-            copy.start()
-
     total_devices = n_year * n_row * n_col
     near = (n_year - 1) + (n_row - 1) <= ITERS
 
@@ -93,14 +82,6 @@
 
     barrier = pltpu.get_barrier_semaphore()
     if near:
-        for other in range(1, n_col):
-            pl.semaphore_signal(
-                barrier,
-                inc=1,
-                device_id=(year, row, lax.rem(col + other, n_col)),
-                device_id_type=MESH,
-            )
-        expected = n_col - 1
         for present, target in (
             (has_prev, (year - 1, row, col)),
             (has_next, (year + 1, row, col)),
@@ -111,12 +92,46 @@
             def _(target=target):
                 pl.semaphore_signal(barrier, inc=1, device_id=target, device_id_type=MESH)
 
+        for other in range(1, n_col):
+            pl.semaphore_signal(
+                barrier,
+                inc=1,
+                device_id=(year, row, lax.rem(col + other, n_col)),
+                device_id_type=MESH,
+            )
+        expected = n_col - 1
+        for present in (has_prev, has_next, has_up, has_down):
             expected = expected + present.astype(jnp.int32)
-        pl.semaphore_wait(barrier, expected)
     else:
         for other in range(1, total_devices):
             pl.semaphore_signal(barrier, inc=1, device_id=peer(other), device_id_type=MESH)
-        pl.semaphore_wait(barrier, total_devices - 1)
+        expected = total_devices - 1
+
+    param_load = pltpu.make_async_copy(
+        params.at[0], field.at[0, 0, :, pl.ds(SUB, rows), :], load_sem.at[0]
+    )
+    small_loads = (
+        pltpu.make_async_copy(land_mask, land, load_sem.at[1]),
+        pltpu.make_async_copy(spatial_weight, spatial, load_sem.at[2]),
+        pltpu.make_async_copy(temporal_weight, temporal, load_sem.at[3]),
+    )
+
+    def input_loads(position):
+        start = chunk_rows(position)
+        where = (slice(None), pl.ds(start, step_rows), slice(None))
+        return (
+            pltpu.make_async_copy(observed.at[0].at[where], obs.at[where], load_sem.at[4 + 2 * position]),
+            pltpu.make_async_copy(quality.at[0].at[where], qual.at[where], load_sem.at[5 + 2 * position]),
+        )
+
+    param_load.start()
+    for copy in small_loads:
+        copy.start()
+    for position in range(chunks):
+        for copy in input_loads(position):
+            copy.start()
+
+    pl.semaphore_wait(barrier, expected)
 
     sides = (
         (has_next, (year + 1, row, col), 1, has_prev),
@@ -131,9 +146,19 @@
         return pltpu.make_async_remote_copy(
             src_ref=field.at[step, 0, :, where, :],
             dst_ref=field.at[step, slot, :, where, :],
-            send_sem=send_sem.at[step, side, position],
+            send_sem=send_sem.at[step, side],
             recv_sem=recv_sem.at[step, side, position],
             device_id=target,
+            device_id_type=MESH,
+        )
+
+    def whole_copy(step, side):
+        return pltpu.make_async_remote_copy(
+            src_ref=field.at[step, 0, :, pl.ds(SUB, rows), :],
+            dst_ref=field.at[step, sides[side][2], :, pl.ds(SUB, rows), :],
+            send_sem=send_sem.at[step, side],
+            recv_sem=recv_sem.at[step, side, 0],
+            device_id=sides[side][1],
             device_id_type=MESH,
         )
 
@@ -150,15 +175,26 @@
             device_id_type=MESH,
         )
 
-    def start_sends(step, position):
-        for side in range(4):
-            @pl.when(sides[side][0])
+    def turn(position, side):
+        return lax.rem(position, 2) == side
+
+    def start_sends(step, position, chosen=range(4), keep=None):
+        for side in chosen:
+            present = sides[side][0]
+            if keep is not None and side < 2:
+                present = jnp.logical_and(present, keep(position, side))
+
+            @pl.when(present)
             def _(side=side):
                 side_copy(step, position, side).start()
 
-    def wait_sides(step, position):
-        for side in range(4):
-            @pl.when(sides[side][3])
+    def wait_sides(step, position, chosen=range(4), keep=None):
+        for side in chosen:
+            present = sides[side][3]
+            if keep is not None and side < 2:
+                present = jnp.logical_and(present, keep(position, side))
+
+            @pl.when(present)
             def _(side=side):
                 side_copy(step, position, side).wait_recv()
 
@@ -211,7 +247,7 @@
     grid_left = lane == jnp.where(has_left, -1, 0)
     grid_right = lane == jnp.where(has_right, -1, cols - 1)
 
-    def around(step, p, start):
+    def plane_sum(step, p, start):
         own = pl.ds(start + SUB, SUB)
         here = field[step, 0, p, own, :]
         above = field[step, 0, p, pl.ds(start, SUB), :]
@@ -224,7 +260,11 @@
         )
         left = jnp.where(grid_left, here, left)
         right = jnp.where(grid_right, here, right)
-        plane = (up + down) + (left + right)
+        return here, (up + down) + (left + right)
+
+    def around(step, p, start):
+        own = pl.ds(start + SUB, SUB)
+        here, plane = plane_sum(step, p, start)
         yearly = field[step, prev_slot, p, own, :] + field[step, next_slot, p, own, :]
         return here, spatial[p] * plane + temporal[p] * yearly
 
@@ -318,29 +358,21 @@
 
     zero = jnp.zeros((SUB, cols), jnp.float32)
 
+    def walk(step, position):
+        return chunk_rows(position), position == 0, position == chunks - 1
+
     def make_stage(stage):
         def body(position, carry):
             odd_sum, even_sum = carry
-            start = chunk_rows(position)
-            first, last = position == 0, position == chunks - 1
-            if stage == 0:
-                for copy in input_loads(position):
-                    copy.wait()
-
-                def each(b, c):
-                    normal(pl.multiple_of(start + b * SUB, SUB))
-                    return c
-
-                lax.fori_loop(0, BLOCKS, each, 0)
-            before = stage
-            wait_sides(before, position)
-            wait_edges(before, first, last)
+            start, first, last = walk(stage, position)
+            wait_sides(stage, position)
+            wait_edges(stage, first, last)
             for b in range(BLOCKS):
                 at = pl.multiple_of(start + b * SUB, SUB)
                 rows_here = pl.ds(at, SUB)
                 held, pushed = [], []
                 for p in range(count):
-                    here, push = around(before, p, at)
+                    here, push = around(stage, p, at)
                     if stage == 0:
                         push = (resid[0, p, rows_here, :] + push) - (
                             4.0 * spatial[p] + 2.0 * temporal[p]
@@ -350,64 +382,103 @@
                     pushed.append(push)
                 if stage > 0:
                     odd_sum = odd_sum + dot(held, pushed)
-                if stage < ITERS:
-                    turned = precondition(at, pushed)
-                    for p in range(count):
-                        field[stage + 1, 0, p, pl.ds(at + SUB, SUB), :] = turned[p]
-                    even_sum = even_sum + dot(turned, pushed)
-            if stage < ITERS:
-                start_sends(stage + 1, position)
-                close_edges(stage + 1, first, last)
+                turned = precondition(at, pushed)
+                for p in range(count):
+                    field[stage + 1, 0, p, pl.ds(at + SUB, SUB), :] = turned[p]
+                even_sum = even_sum + dot(turned, pushed)
+            start_sends(stage + 1, position, keep=turn if stage + 1 == ITERS else None)
+            close_edges(stage + 1, first, last)
             return odd_sum, even_sum
 
         return body
 
+    for copy in small_loads:
+        copy.wait()
+
+    first_stage = make_stage(0)
+
+    def opening(position, carry):
+        @pl.when(position < chunks)
+        def _():
+            for copy in input_loads(position):
+                copy.wait()
+            for b in range(BLOCKS):
+                normal(pl.multiple_of(chunk_rows(position) + b * SUB, SUB))
+
+        return lax.cond(
+            position >= LEAD, lambda c: first_stage(position - LEAD, c), lambda c: c, carry
+        )
+
     sums = []
-    for stage in range(ITERS + 1):
-        odd_sum, even_sum = lax.fori_loop(0, chunks, make_stage(stage), (zero, zero))
-        if stage > 0:
+    for stage in range(ITERS):
+        if stage == 0:
+            odd_sum, even_sum = lax.fori_loop(0, chunks + LEAD, opening, (zero, zero))
+        else:
+            odd_sum, even_sum = lax.fori_loop(0, chunks, make_stage(stage), (zero, zero))
             sums.append(odd_sum)
-        if stage < ITERS:
-            sums.append(even_sum)
+        sums.append(even_sum)
+
+    others = total_devices - 1
+
+    def sum_copy(note, other):
+        return pltpu.make_async_remote_copy(
+            src_ref=notes.at[note, pl.ds(0, 1)],
+            dst_ref=slots.at[note, pl.ds(other - 1, 1)],
+            send_sem=sum_send.at[note, other - 1],
+            recv_sem=sum_recv.at[note, other - 1],
+            device_id=peer(other),
+            device_id_type=MESH,
+        )
+
+    def gather(note):
+        for other in range(1, total_devices):
+            sum_copy(note, other).wait_recv()
+        return jnp.sum(slots[note], axis=0, keepdims=True) + notes[note, 0:1, :]
 
     for at, value in enumerate(sums):
         moments[at : at + 1, :] = jnp.sum(value, axis=0, keepdims=True)
-
-    def sum_copy(other):
-        return pltpu.make_async_remote_copy(
-            src_ref=moments,
-            dst_ref=slots.at[other - 1],
-            send_sem=sum_send.at[other - 1],
-            recv_sem=sum_recv.at[other - 1],
-            device_id=peer(other),
-            device_id_type=MESH,
-        )
-
+    moments[len(sums) : SUB, :] = jnp.zeros((SUB - len(sums), cols), jnp.float32)
+    folded = jnp.broadcast_to(jnp.sum(moments[...], axis=1, keepdims=True), (SUB, cols))
+    notes[0, 0:1, :] = jnp.sum(jnp.where(lane == level, folded, 0.0), axis=0, keepdims=True)
     for other in range(1, total_devices):
-        sum_copy(other).start()
-    for step in range(ROUNDS):
-        def drain(position, carry, step=step):
-            for side in range(4):
-                @pl.when(sides[side][0])
-                def _(side=side):
-                    side_copy(step, position, side).wait_send()
-            return carry
-
-        lax.fori_loop(0, chunks, drain, 0)
-        for at_last, present in ((False, has_first), (True, has_last)):
-            @pl.when(present)
-            def _(at_last=at_last, step=step):
-                row_copy(step, at_last).wait_send()
-    parts = [moments[...]]
+        sum_copy(0, other).start()
+
+    def send_rest(position, carry):
+        start_sends(ITERS, position, (0, 1), lambda at, side: ~turn(at, side))
+        return carry
+
+    lax.fori_loop(0, chunks, send_rest, 0)
+
+    def closing(position, last_sum):
+        start, first, last = walk(ITERS, position)
+        later = turn(position, 0)
+        slot = jnp.where(later, prev_slot, next_slot)
+        twice = jnp.where(jnp.where(later, has_prev, has_next), 2.0, 1.0)
+        alone = jnp.where(jnp.where(later, has_next, has_prev), 0.0, 1.0)
+        wait_sides(ITERS, position, keep=turn)
+        wait_edges(ITERS, first, last)
+        for b in range(BLOCKS):
+            at = pl.multiple_of(start + b * SUB, SUB)
+            held, pushed = [], []
+            for p in range(count):
+                here, plane = plane_sum(ITERS, p, at)
+                beside = field[ITERS, slot, p, pl.ds(at + SUB, SUB), :]
+                plane = spatial[p] * plane
+                resid[ITERS, p, pl.ds(at, SUB), :] = plane + temporal[p] * beside
+                held.append(here)
+                pushed.append(plane + temporal[p] * (twice * beside + alone * here))
+            last_sum = last_sum + dot(held, pushed)
+        return last_sum
+
+    last_sum = lax.fori_loop(0, chunks, closing, zero)
+    notes[1, 0:1, :] = jnp.sum(last_sum, axis=0, keepdims=True)
     for other in range(1, total_devices):
-        sum_copy(other).wait_recv()
-        parts.append(slots[other - 1])
-    while len(parts) > 1:
-        parts = [sum(parts[i : i + 2][1:], parts[i]) for i in range(0, len(parts), 2)]
-    total = parts[0]
-    total = jnp.broadcast_to(jnp.sum(total, axis=1, keepdims=True), total.shape)
-    mu = [total[at : at + 1, :] for at in range(2 * ITERS)]
-    drop = [mu[at] - mu[at + 1] for at in range(2 * ITERS - 1)]
+        sum_copy(1, other).start()
+
+    known = jnp.where(lane == level, jnp.broadcast_to(gather(0), (SUB, cols)), 0.0)
+    known = jnp.broadcast_to(jnp.sum(known, axis=1, keepdims=True), (SUB, cols))
+    mu = [known[at : at + 1, :] for at in range(2 * ITERS - 1)]
+    drop = [mu[at] - mu[at + 1] for at in range(2 * ITERS - 2)]
 
     def form(coefs, table):
         total = None
@@ -422,53 +493,115 @@
     search, direction = [one], [one]
     lengths = [jnp.zeros_like(one)] * ITERS
     inner = mu[0]
-    for sweep in range(ITERS):
+    for sweep in range(ITERS - 1):
         alpha = inner / form(direction, drop)
         for j in range(sweep + 1):
             lengths[j] = lengths[j] + alpha * direction[j]
-        if sweep + 1 < ITERS:
-            grown = []
-            for j in range(sweep + 2):
-                change = None
-                if j <= sweep:
-                    change = direction[j]
-                if j > 0:
-                    change = -direction[j - 1] if change is None else change - direction[j - 1]
-                base = search[j] if j <= sweep else None
-                grown.append(-alpha * change if base is None else base - alpha * change)
-            search = grown
-            fresh = form(search, mu)
-            ratio = fresh / inner
-            inner = fresh
-            direction = [
-                search[j] + ratio * direction[j] if j <= sweep else search[j]
-                for j in range(sweep + 2)
-            ]
-
-    steps = [jnp.broadcast_to(value, (SUB, cols)) for value in lengths]
-    mixes = [1.0 - steps[0]]
-    mixes += [steps[j - 1] - steps[j] for j in range(1, ITERS)]
-    mixes += [steps[-1]]
+        grown = []
+        for j in range(sweep + 2):
+            change = None
+            if j <= sweep:
+                change = direction[j]
+            if j > 0:
+                change = -direction[j - 1] if change is None else change - direction[j - 1]
+            base = search[j] if j <= sweep else None
+            grown.append(-alpha * change if base is None else base - alpha * change)
+        search = grown
+        fresh = form(search, mu)
+        ratio = fresh / inner
+        inner = fresh
+        direction = [
+            search[j] + ratio * direction[j] if j <= sweep else search[j]
+            for j in range(sweep + 2)
+        ]
+    curve = form(direction, drop + [mu[-1]])
+    bend = direction[-1] * direction[-1]
+
+    def wide(values):
+        return [jnp.broadcast_to(value, (SUB, cols)) for value in values]
+
+    def mixes(values, head):
+        return wide(
+            [head - values[0]]
+            + [values[j - 1] - values[j] for j in range(1, ITERS)]
+            + [values[-1]]
+        )
+
+    paces, steers = wide(lengths[:-1]), wide(direction)
+    base_mix, slope_mix = mixes(lengths, 1.0)[:-1], mixes(direction, 0.0)
+
+    def prepare(position, carry):
+        start, _, _ = walk(ITERS, position)
+        slot = jnp.where(turn(position, 0), next_slot, prev_slot)
+        wait_sides(ITERS, position, (0, 1), lambda at, side: ~turn(at, side))
+        for b in range(BLOCKS):
+            at = pl.multiple_of(start + b * SUB, SUB)
+            rows_here, padded = pl.ds(at, SUB), pl.ds(at + SUB, SUB)
+            for p in range(count):
+                vectors = [field[j + 1, 0, p, padded, :] for j in range(ITERS)]
+                total = field[0, 0, p, padded, :]
+                for pace, vector in zip(paces, vectors):
+                    total = total + pace * vector
+                new_params[0, p, rows_here, :] = total
+                total = steers[0] * vectors[0]
+                for steer, vector in zip(steers[1:], vectors[1:]):
+                    total = total + steer * vector
+                slope[0, p, rows_here, :] = total
+                vectors = [resid[j, p, rows_here, :] for j in range(ITERS + 1)]
+                vectors[-1] = vectors[-1] + temporal[p] * field[ITERS, slot, p, padded, :]
+                total = base_mix[0] * vectors[0]
+                for mix, vector in zip(base_mix[1:], vectors[1:]):
+                    total = total + mix * vector
+                residual[0, p, rows_here, :] = total
+                total = slope_mix[0] * vectors[0]
+                for mix, vector in zip(slope_mix[1:], vectors[1:]):
+                    total = total + mix * vector
+                slope[1, p, rows_here, :] = total
+        return carry
+
+    lax.fori_loop(0, chunks, prepare, 0)
+
+    for step in range(ROUNDS):
+        for side in range(4):
+            @pl.when(sides[side][0])
+            def _(side=side, step=step):
+                whole_copy(step, side).wait_send()
+        for at_last, present in ((False, has_first), (True, has_last)):
+            @pl.when(present)
+            def _(at_last=at_last, step=step):
+                row_copy(step, at_last).wait_send()
+    for other in range(1, total_devices):
+        sum_copy(0, other).wait_send()
+
+    final = jnp.broadcast_to(jnp.sum(gather(1), axis=1, keepdims=True), (1, cols))
+    alpha = jnp.broadcast_to(inner / (curve - bend * final), (SUB, cols))
 
     def finish(b, carry):
-        at = pl.multiple_of(b * SUB, SUB)
-        rows_here = pl.ds(at, SUB)
-        padded = pl.ds(at + SUB, SUB)
+        rows_here = pl.ds(pl.multiple_of(b * SUB, SUB), SUB)
         for p in range(count):
-            total = field[0, 0, p, padded, :]
-            for j in range(ITERS):
-                total = total + steps[j] * field[j + 1, 0, p, padded, :]
-            new_params[0, p, rows_here, :] = total
-            total = mixes[0] * resid[0, p, rows_here, :]
-            for j in range(1, ITERS + 1):
-                total = total + mixes[j] * resid[j, p, rows_here, :]
-            residual[0, p, rows_here, :] = total
+            new_params[0, p, rows_here, :] = (
+                new_params[0, p, rows_here, :] + alpha * slope[0, p, rows_here, :]
+            )
+            residual[0, p, rows_here, :] = (
+                residual[0, p, rows_here, :] + alpha * slope[1, p, rows_here, :]
+            )
         return carry
 
     lax.fori_loop(0, rows // SUB, finish, 0)
 
     for other in range(1, total_devices):
-        sum_copy(other).wait_send()
+        sum_copy(1, other).wait_send()
+
+
+def store_kernel(new_params, residual, new_params_out, residual_out, sem):
+    copies = (
+        pltpu.make_async_copy(new_params, new_params_out, sem.at[0]),
+        pltpu.make_async_copy(residual, residual_out, sem.at[1]),
+    )
+    for copy in copies:
+        copy.start()
+    for copy in copies:
+        copy.wait()
 
 
 def per_device(sizes, observed, quality, land_mask, params, spatial_weight, temporal_weight):
@@ -480,37 +613,55 @@
     f32 = jnp.float32
     vmem = pl.BlockSpec(memory_space=pltpu.VMEM)
     hbm = pl.BlockSpec(memory_space=pltpu.HBM)
-    smem = pl.BlockSpec(memory_space=pltpu.SMEM)
     dma = pltpu.SemaphoreType.DMA
-    return pl.pallas_call(
+    outs = (jax.ShapeDtypeStruct(params.shape, f32), jax.ShapeDtypeStruct(params.shape, f32))
+    results = pl.pallas_call(
         functools.partial(kernel, sizes),
-        out_shape=(
-            jax.ShapeDtypeStruct(params.shape, f32),
-            jax.ShapeDtypeStruct(params.shape, f32),
-        ),
-        in_specs=[hbm, hbm, vmem, hbm, smem, smem],
+        out_shape=outs,
+        in_specs=[hbm] * 6,
         out_specs=(vmem, vmem),
         scratch_shapes=[
             pltpu.VMEM((dates, rows, cols), f32),
             pltpu.VMEM((dates, rows, cols), jnp.int32),
+            pltpu.VMEM((rows, cols), jnp.int32),
+            pltpu.SMEM((count,), f32),
+            pltpu.SMEM((count,), f32),
             pltpu.VMEM((ROUNDS, 5, count, rows + 2 * SUB, cols), f32),
             pltpu.VMEM((count * (count + 1) // 2, rows, cols), f32),
             pltpu.VMEM((ROUNDS, count, rows, cols), f32),
-            pltpu.VMEM((2 * ITERS, cols), f32),
-            pltpu.VMEM((max(others, 1), 2 * ITERS, cols), f32),
-            dma((1 + 2 * chunks,)),
-            dma((ROUNDS, 4, chunks)),
+            pltpu.VMEM((2, count, rows, cols), f32),
+            pltpu.VMEM((SUB, cols), f32),
+            pltpu.VMEM((2, SUB, cols), f32),
+            pltpu.VMEM((2, max(others, 1), cols), f32),
+            dma((4 + 2 * chunks,)),
+            dma((ROUNDS, 4)),
             dma((ROUNDS, 4, chunks)),
             dma((ROUNDS, 2)),
             dma((ROUNDS, 2)),
-            dma((max(others, 1),)),
-            dma((max(others, 1),)),
+            dma((2, max(others, 1))),
+            dma((2, max(others, 1))),
         ],
         compiler_params=pltpu.CompilerParams(
-            collective_id=0, has_side_effects=True, vmem_limit_bytes=67043328
+            collective_id=0, has_side_effects=True, vmem_limit_bytes=24 * 2**20
         ),
         name="gauss_newton",
-    )(observed, quality, land_mask, params, spatial_weight, temporal_weight)
+    )(
+        *[
+            pltpu.with_memory_space_constraint(operand, pltpu.HBM)
+            for operand in (
+                observed, quality, land_mask, params, spatial_weight, temporal_weight
+            )
+        ]
+    )
+    return pl.pallas_call(
+        store_kernel,
+        out_shape=outs,
+        in_specs=[vmem, vmem],
+        out_specs=(hbm, hbm),
+        scratch_shapes=[dma((2,))],
+        compiler_params=pltpu.CompilerParams(vmem_limit_bytes=2**20),
+        name="store",
+    )(*results)
 
 
 def solution(mesh):

time: 44.5 us -> 39.6 us (0.89)
  local copies, waits for them, and re-layouts: 3.28 us -> 0 us
  Pallas kernels: 40.4 us -> 38.8 us
    unnamed x2 -> x0, local copies, waits for them, and re-layouts: 3.28 us -> none
    pallas_call x1 -> x2, Pallas kernels: 40.4 us -> 38.8 us  [the longest x1 38 us: per_device(): pl.pallas_call(functools.partial(kernel, sizes), out_shape=outs, in_specs...]
where the time goes in v1:
time: 39.6 us; the launch traced here: 39.4 us
  Pallas kernels  38.8 us (98%)
  between operations  0.64 us (2%)
    pallas_call x1, Pallas kernels, per_device(): pl.pallas_call(functools.partial(kernel, sizes), out_shape=outs, in_specs...  38 us

profile of v1, /device:TPU:0, one launch (start us, length us, event | category | flops | bytes accessed | tf_op | source)
XLA Modules:
  0.0 39.4 jit_solution(8116968861164268201)
XLA Ops:
  0.6 38.0 %gauss_newton.1 = (f32[1,7,64,128]{3,2,1,0:T(8,128)S(1)}, f32[1,7,64,128]{3,2,1,0:T(8,128)S(1)}) custom-call(f32[1,46,64,128]{3,2,1,0:T(8,128)} %observed.1, s32[1,46,64,128]{3,2,1,0:T(8,128)} %quality.1, s32[64,128]{1,0:T(8,128)} %land_mask.1, f32[1,7,64,128]{3,2,1,0:T(8,128)} %params.1, f32[7]{0:T(128)} %spatial_weight.1, f32[7]{0:T(128)} %temporal_weight.1), custom_call_target="tpu_custom_call" | custom-call | tf_op jit(solution)/shard_map/gauss_newton/pallas_call | solution.py:618
  38.7 0.8 %store.1 = (f32[1,7,64,128]{3,2,1,0:T(8,128)}, f32[1,7,64,128]{3,2,1,0:T(8,128)}) custom-call(f32[1,7,64,128]{3,2,1,0:T(8,128)S(1)} %get-tuple-element.4.new_params, f32[1,7,64,128]{3,2,1,0:T(8,128)S(1)} %get-tuple-element.5.residual), custom_call_target="tpu_custom_call" | custom-call | tf_op jit(solution)/shard_map/store/pallas_call | solution.py:656

commit v2 on v1

--- a/solution.py
+++ b/solution.py
@@ -10,8 +10,8 @@
 ITERS = 4
 ROUNDS = ITERS + 1
 SUB = 8
-BLOCKS = 1
 LEAD = 2
+PAIR = 2
 DAMPING = 0.1
 MESH = pl.DeviceIdType.MESH
 
@@ -44,7 +44,8 @@
     slots,
     load_sem,
     send_sem,
-    recv_sem,
+    year_recv,
+    col_recv,
     row_send,
     row_recv,
     sum_send,
@@ -53,8 +54,8 @@
     n_year, n_row, n_col = sizes
     dates, rows, cols = obs.shape
     count = resid.shape[1]
-    step_rows = SUB * BLOCKS
-    chunks = rows // step_rows
+    chunks = rows // SUB
+    wide_rows = SUB * PAIR
     pairs = pairs_of(count)
     place = {pair: at for at, pair in enumerate(pairs)}
 
@@ -71,7 +72,11 @@
 
     def chunk_rows(position):
         chunk = jnp.where(even, position, chunks - 1 - position)
-        return pl.multiple_of(chunk * step_rows, step_rows)
+        return pl.multiple_of(chunk * SUB, SUB)
+
+    def wide_start(group):
+        group = jnp.where(even, group, chunks // PAIR - 1 - group)
+        return pl.multiple_of(group * wide_rows, wide_rows)
 
     total_devices = n_year * n_row * n_col
     near = (n_year - 1) + (n_row - 1) <= ITERS
@@ -116,19 +121,18 @@
         pltpu.make_async_copy(temporal_weight, temporal, load_sem.at[3]),
     )
 
-    def input_loads(position):
-        start = chunk_rows(position)
-        where = (slice(None), pl.ds(start, step_rows), slice(None))
+    def input_loads(group):
+        where = (slice(None), pl.ds(wide_start(group), wide_rows), slice(None))
         return (
-            pltpu.make_async_copy(observed.at[0].at[where], obs.at[where], load_sem.at[4 + 2 * position]),
-            pltpu.make_async_copy(quality.at[0].at[where], qual.at[where], load_sem.at[5 + 2 * position]),
+            pltpu.make_async_copy(observed.at[0].at[where], obs.at[where], load_sem.at[4 + 2 * group]),
+            pltpu.make_async_copy(quality.at[0].at[where], qual.at[where], load_sem.at[5 + 2 * group]),
         )
 
     param_load.start()
     for copy in small_loads:
         copy.start()
-    for position in range(chunks):
-        for copy in input_loads(position):
+    for group in range(chunks // PAIR):
+        for copy in input_loads(group):
             copy.start()
 
     pl.semaphore_wait(barrier, expected)
@@ -142,36 +146,59 @@
 
     def side_copy(step, position, side):
         _, target, slot, _ = sides[side]
-        where = pl.ds(chunk_rows(position) + SUB, step_rows)
+        if side < 2:
+            where = pl.ds(chunk_rows(position) + SUB, SUB)
+            landing = year_recv.at[step % 2, side, position]
+        else:
+            group = position // PAIR
+            where = pl.ds(pl.multiple_of(wide_start(group) + SUB, SUB), wide_rows)
+            landing = col_recv.at[step % 2, side - 2, group]
         return pltpu.make_async_remote_copy(
             src_ref=field.at[step, 0, :, where, :],
             dst_ref=field.at[step, slot, :, where, :],
-            send_sem=send_sem.at[step, side],
-            recv_sem=recv_sem.at[step, side, position],
+            send_sem=send_sem.at[side],
+            recv_sem=landing,
             device_id=target,
             device_id_type=MESH,
         )
 
-    def whole_copy(step, side):
-        return pltpu.make_async_remote_copy(
-            src_ref=field.at[step, 0, :, pl.ds(SUB, rows), :],
-            dst_ref=field.at[step, sides[side][2], :, pl.ds(SUB, rows), :],
-            send_sem=send_sem.at[step, side],
-            recv_sem=recv_sem.at[step, side, 0],
-            device_id=sides[side][1],
-            device_id_type=MESH,
-        )
-
-    def row_copy(step, last):
+    def row_spot(last):
         top = jnp.logical_xor(even, last)
         source = pl.multiple_of(jnp.where(top, SUB, rows), SUB)
         target = pl.multiple_of(jnp.where(top, rows + SUB, 0), SUB)
+        return source, target, (year, toward_last if last else toward_first, col)
+
+    def row_copy(step, last):
+        source, target, device = row_spot(last)
         return pltpu.make_async_remote_copy(
             src_ref=field.at[step, 0, :, pl.ds(source, SUB), :],
             dst_ref=field.at[step, 0, :, pl.ds(target, SUB), :],
-            send_sem=row_send.at[step, int(last)],
-            recv_sem=row_recv.at[step, int(last)],
-            device_id=(year, toward_last if last else toward_first, col),
+            send_sem=row_send.at[int(last)],
+            recv_sem=row_recv.at[step % 2, int(last)],
+            device_id=device,
+            device_id_type=MESH,
+        )
+
+    def side_sends(side):
+        where = (slice(None), 0, slice(None), pl.ds(SUB, rows), slice(None))
+        return pltpu.make_async_remote_copy(
+            src_ref=field.at[where],
+            dst_ref=field.at[where],
+            send_sem=send_sem.at[side],
+            recv_sem=send_sem.at[side],
+            device_id=sides[side][1],
+            device_id_type=MESH,
+        )
+
+    def row_sends(last):
+        source, _, device = row_spot(last)
+        where = (slice(None), 0, slice(None), pl.ds(source, SUB), slice(None))
+        return pltpu.make_async_remote_copy(
+            src_ref=field.at[where],
+            dst_ref=field.at[where],
+            send_sem=row_send.at[int(last)],
+            recv_sem=row_send.at[int(last)],
+            device_id=device,
             device_id_type=MESH,
         )
 
@@ -181,7 +208,10 @@
     def start_sends(step, position, chosen=range(4), keep=None):
         for side in chosen:
             present = sides[side][0]
-            if keep is not None and side < 2:
+            if side >= 2:
+                ready = lax.rem(position, PAIR) == PAIR - 1
+                present = jnp.logical_and(present, ready)
+            elif keep is not None:
                 present = jnp.logical_and(present, keep(position, side))
 
             @pl.when(present)
@@ -191,7 +221,9 @@
     def wait_sides(step, position, chosen=range(4), keep=None):
         for side in chosen:
             present = sides[side][3]
-            if keep is not None and side < 2:
+            if side >= 2:
+                present = jnp.logical_and(present, lax.rem(position, PAIR) == 0)
+            elif keep is not None:
                 present = jnp.logical_and(present, keep(position, side))
 
             @pl.when(present)
@@ -358,34 +390,32 @@
 
     zero = jnp.zeros((SUB, cols), jnp.float32)
 
-    def walk(step, position):
+    def walk(position):
         return chunk_rows(position), position == 0, position == chunks - 1
 
     def make_stage(stage):
         def body(position, carry):
             odd_sum, even_sum = carry
-            start, first, last = walk(stage, position)
+            start, first, last = walk(position)
             wait_sides(stage, position)
             wait_edges(stage, first, last)
-            for b in range(BLOCKS):
-                at = pl.multiple_of(start + b * SUB, SUB)
-                rows_here = pl.ds(at, SUB)
-                held, pushed = [], []
-                for p in range(count):
-                    here, push = around(stage, p, at)
-                    if stage == 0:
-                        push = (resid[0, p, rows_here, :] + push) - (
-                            4.0 * spatial[p] + 2.0 * temporal[p]
-                        ) * here
-                    resid[stage, p, rows_here, :] = push
-                    held.append(here)
-                    pushed.append(push)
-                if stage > 0:
-                    odd_sum = odd_sum + dot(held, pushed)
-                turned = precondition(at, pushed)
-                for p in range(count):
-                    field[stage + 1, 0, p, pl.ds(at + SUB, SUB), :] = turned[p]
-                even_sum = even_sum + dot(turned, pushed)
+            rows_here = pl.ds(start, SUB)
+            held, pushed = [], []
+            for p in range(count):
+                here, push = around(stage, p, start)
+                if stage == 0:
+                    push = (resid[0, p, rows_here, :] + push) - (
+                        4.0 * spatial[p] + 2.0 * temporal[p]
+                    ) * here
+                resid[stage, p, rows_here, :] = push
+                held.append(here)
+                pushed.append(push)
+            if stage > 0:
+                odd_sum = odd_sum + dot(held, pushed)
+            turned = precondition(start, pushed)
+            for p in range(count):
+                field[stage + 1, 0, p, pl.ds(start + SUB, SUB), :] = turned[p]
+            even_sum = even_sum + dot(turned, pushed)
             start_sends(stage + 1, position, keep=turn if stage + 1 == ITERS else None)
             close_edges(stage + 1, first, last)
             return odd_sum, even_sum
@@ -400,10 +430,12 @@
     def opening(position, carry):
         @pl.when(position < chunks)
         def _():
-            for copy in input_loads(position):
-                copy.wait()
-            for b in range(BLOCKS):
-                normal(pl.multiple_of(chunk_rows(position) + b * SUB, SUB))
+            @pl.when(lax.rem(position, PAIR) == 0)
+            def _():
+                for copy in input_loads(position // PAIR):
+                    copy.wait()
+
+            normal(chunk_rows(position))
 
         return lax.cond(
             position >= LEAD, lambda c: first_stage(position - LEAD, c), lambda c: c, carry
@@ -424,15 +456,24 @@
         return pltpu.make_async_remote_copy(
             src_ref=notes.at[note, pl.ds(0, 1)],
             dst_ref=slots.at[note, pl.ds(other - 1, 1)],
-            send_sem=sum_send.at[note, other - 1],
-            recv_sem=sum_recv.at[note, other - 1],
+            send_sem=sum_send.at[note],
+            recv_sem=sum_recv.at[note],
             device_id=peer(other),
             device_id_type=MESH,
         )
 
+    def sum_copies(note):
+        return pltpu.make_async_remote_copy(
+            src_ref=slots.at[note],
+            dst_ref=slots.at[note],
+            send_sem=sum_send.at[note],
+            recv_sem=sum_recv.at[note],
+            device_id=peer(1),
+            device_id_type=MESH,
+        )
+
     def gather(note):
-        for other in range(1, total_devices):
-            sum_copy(note, other).wait_recv()
+        sum_copies(note).wait_recv()
         return jnp.sum(slots[note], axis=0, keepdims=True) + notes[note, 0:1, :]
 
     for at, value in enumerate(sums):
@@ -450,24 +491,22 @@
     lax.fori_loop(0, chunks, send_rest, 0)
 
     def closing(position, last_sum):
-        start, first, last = walk(ITERS, position)
+        start, first, last = walk(position)
         later = turn(position, 0)
         slot = jnp.where(later, prev_slot, next_slot)
         twice = jnp.where(jnp.where(later, has_prev, has_next), 2.0, 1.0)
         alone = jnp.where(jnp.where(later, has_next, has_prev), 0.0, 1.0)
         wait_sides(ITERS, position, keep=turn)
         wait_edges(ITERS, first, last)
-        for b in range(BLOCKS):
-            at = pl.multiple_of(start + b * SUB, SUB)
-            held, pushed = [], []
-            for p in range(count):
-                here, plane = plane_sum(ITERS, p, at)
-                beside = field[ITERS, slot, p, pl.ds(at + SUB, SUB), :]
-                plane = spatial[p] * plane
-                resid[ITERS, p, pl.ds(at, SUB), :] = plane + temporal[p] * beside
-                held.append(here)
-                pushed.append(plane + temporal[p] * (twice * beside + alone * here))
-            last_sum = last_sum + dot(held, pushed)
+        held, pushed = [], []
+        for p in range(count):
+            here, plane = plane_sum(ITERS, p, start)
+            beside = field[ITERS, slot, p, pl.ds(start + SUB, SUB), :]
+            plane = spatial[p] * plane
+            resid[ITERS, p, pl.ds(start, SUB), :] = plane + temporal[p] * beside
+            held.append(here)
+            pushed.append(plane + temporal[p] * (twice * beside + alone * here))
+        last_sum = last_sum + dot(held, pushed)
         return last_sum
 
     last_sum = lax.fori_loop(0, chunks, closing, zero)
@@ -531,47 +570,45 @@
     base_mix, slope_mix = mixes(lengths, 1.0)[:-1], mixes(direction, 0.0)
 
     def prepare(position, carry):
-        start, _, _ = walk(ITERS, position)
+        start, _, _ = walk(position)
         slot = jnp.where(turn(position, 0), next_slot, prev_slot)
         wait_sides(ITERS, position, (0, 1), lambda at, side: ~turn(at, side))
-        for b in range(BLOCKS):
-            at = pl.multiple_of(start + b * SUB, SUB)
-            rows_here, padded = pl.ds(at, SUB), pl.ds(at + SUB, SUB)
-            for p in range(count):
-                vectors = [field[j + 1, 0, p, padded, :] for j in range(ITERS)]
-                total = field[0, 0, p, padded, :]
-                for pace, vector in zip(paces, vectors):
-                    total = total + pace * vector
-                new_params[0, p, rows_here, :] = total
-                total = steers[0] * vectors[0]
-                for steer, vector in zip(steers[1:], vectors[1:]):
-                    total = total + steer * vector
-                slope[0, p, rows_here, :] = total
-                vectors = [resid[j, p, rows_here, :] for j in range(ITERS + 1)]
-                vectors[-1] = vectors[-1] + temporal[p] * field[ITERS, slot, p, padded, :]
-                total = base_mix[0] * vectors[0]
-                for mix, vector in zip(base_mix[1:], vectors[1:]):
-                    total = total + mix * vector
-                residual[0, p, rows_here, :] = total
-                total = slope_mix[0] * vectors[0]
-                for mix, vector in zip(slope_mix[1:], vectors[1:]):
-                    total = total + mix * vector
-                slope[1, p, rows_here, :] = total
+        rows_here, padded = pl.ds(start, SUB), pl.ds(start + SUB, SUB)
+        for p in range(count):
+            vectors = [field[j + 1, 0, p, padded, :] for j in range(ITERS)]
+            total = field[0, 0, p, padded, :]
+            for pace, vector in zip(paces, vectors):
+                total = total + pace * vector
+            new_params[0, p, rows_here, :] = total
+            total = steers[0] * vectors[0]
+            for steer, vector in zip(steers[1:], vectors[1:]):
+                total = total + steer * vector
+            slope[0, p, rows_here, :] = total
+            vectors = [resid[j, p, rows_here, :] for j in range(ITERS + 1)]
+            vectors[-1] = vectors[-1] + temporal[p] * field[ITERS, slot, p, padded, :]
+            total = base_mix[0] * vectors[0]
+            for mix, vector in zip(base_mix[1:], vectors[1:]):
+                total = total + mix * vector
+            residual[0, p, rows_here, :] = total
+            total = slope_mix[0] * vectors[0]
+            for mix, vector in zip(slope_mix[1:], vectors[1:]):
+                total = total + mix * vector
+            slope[1, p, rows_here, :] = total
         return carry
 
     lax.fori_loop(0, chunks, prepare, 0)
 
-    for step in range(ROUNDS):
-        for side in range(4):
-            @pl.when(sides[side][0])
-            def _(side=side, step=step):
-                whole_copy(step, side).wait_send()
-        for at_last, present in ((False, has_first), (True, has_last)):
-            @pl.when(present)
-            def _(at_last=at_last, step=step):
-                row_copy(step, at_last).wait_send()
-    for other in range(1, total_devices):
-        sum_copy(0, other).wait_send()
+    for side in range(4):
+        @pl.when(sides[side][0])
+        def _(side=side):
+            side_sends(side).wait_send()
+
+    for at_last, present in ((False, has_first), (True, has_last)):
+        @pl.when(present)
+        def _(at_last=at_last):
+            row_sends(at_last).wait_send()
+
+    sum_copies(0).wait_send()
 
     final = jnp.broadcast_to(jnp.sum(gather(1), axis=1, keepdims=True), (1, cols))
     alpha = jnp.broadcast_to(inner / (curve - bend * final), (SUB, cols))
@@ -589,8 +626,7 @@
 
     lax.fori_loop(0, rows // SUB, finish, 0)
 
-    for other in range(1, total_devices):
-        sum_copy(1, other).wait_send()
+    sum_copies(1).wait_send()
 
 
 def store_kernel(new_params, residual, new_params_out, residual_out, sem):
@@ -608,7 +644,8 @@
     n_year, n_row, n_col = sizes
     _, dates, rows, cols = observed.shape
     count = params.shape[1]
-    chunks = rows // (SUB * BLOCKS)
+    chunks = rows // SUB
+    groups = chunks // PAIR
     others = n_year * n_row * n_col - 1
     f32 = jnp.float32
     vmem = pl.BlockSpec(memory_space=pltpu.VMEM)
@@ -633,13 +670,14 @@
             pltpu.VMEM((SUB, cols), f32),
             pltpu.VMEM((2, SUB, cols), f32),
             pltpu.VMEM((2, max(others, 1), cols), f32),
-            dma((4 + 2 * chunks,)),
-            dma((ROUNDS, 4)),
-            dma((ROUNDS, 4, chunks)),
-            dma((ROUNDS, 2)),
-            dma((ROUNDS, 2)),
-            dma((2, max(others, 1))),
-            dma((2, max(others, 1))),
+            dma((4 + 2 * groups,)),
+            dma((4,)),
+            dma((2, 2, chunks)),
+            dma((2, 2, groups)),
+            dma((2,)),
+            dma((2, 2)),
+            dma((2,)),
+            dma((2,)),
         ],
         compiler_params=pltpu.CompilerParams(
             collective_id=0, has_side_effects=True, vmem_limit_bytes=24 * 2**20

time: 39.6 us -> 37.1 us (0.937)
  Pallas kernels: 38.8 us -> 36.3 us
    pallas_call x1, Pallas kernels: 38 us -> 35.5 us  [per_device(): pl.pallas_call(functools.partial(kernel, sizes), out_shape=outs, in_specs...]
where the time goes in v2:
time: 37.1 us; the launch traced here: 37 us
  Pallas kernels  36.3 us (98%)
  between operations  0.64 us (2%)
    pallas_call x1, Pallas kernels, per_device(): pl.pallas_call(functools.partial(kernel, sizes), out_shape=outs, in_specs...  35.5 us
    pallas_call x1, Pallas kernels, per_device(): pl.pallas_call(store_kernel, out_shape=outs, in_specs=[vmem, vmem], out_s...  0.78 us

profile of v2, /device:TPU:0, one launch (start us, length us, event | category | flops | bytes accessed | tf_op | source)
XLA Modules:
  0.0 37.0 jit_solution(11672718144253437823)
XLA Ops:
  0.6 35.5 %gauss_newton.1 = (f32[1,7,64,128]{3,2,1,0:T(8,128)S(1)}, f32[1,7,64,128]{3,2,1,0:T(8,128)S(1)}) custom-call(f32[1,46,64,128]{3,2,1,0:T(8,128)} %observed.1, s32[1,46,64,128]{3,2,1,0:T(8,128)} %quality.1, s32[64,128]{1,0:T(8,128)} %land_mask.1, f32[1,7,64,128]{3,2,1,0:T(8,128)} %params.1, f32[7]{0:T(128)} %spatial_weight.1, f32[7]{0:T(128)} %temporal_weight.1), custom_call_target="tpu_custom_call" | custom-call | tf_op jit(solution)/shard_map/gauss_newton/pallas_call | solution.py:655
  36.2 0.8 %store.1 = (f32[1,7,64,128]{3,2,1,0:T(8,128)}, f32[1,7,64,128]{3,2,1,0:T(8,128)}) custom-call(f32[1,7,64,128]{3,2,1,0:T(8,128)S(1)} %get-tuple-element.4.new_params, f32[1,7,64,128]{3,2,1,0:T(8,128)S(1)} %get-tuple-element.5.residual), custom_call_target="tpu_custom_call" | custom-call | tf_op jit(solution)/shard_map/store/pallas_call | solution.py:694

commit v3 on v2

--- a/solution.py
+++ b/solution.py
@@ -12,6 +12,7 @@
 SUB = 8
 LEAD = 2
 PAIR = 2
+LEVEL = (1, 2, 3)
 DAMPING = 0.1
 MESH = pl.DeviceIdType.MESH
 
@@ -28,8 +29,9 @@
     params,
     spatial_weight,
     temporal_weight,
-    new_params,
-    residual,
+    anchor,
+    slope,
+    pace,
     obs,
     qual,
     land,
@@ -38,7 +40,6 @@
     field,
     inverse,
     resid,
-    slope,
     moments,
     notes,
     slots,
@@ -46,10 +47,12 @@
     send_sem,
     year_recv,
     col_recv,
+    rest_recv,
     row_send,
     row_recv,
     sum_send,
     sum_recv,
+    level_sem,
 ):
     n_year, n_row, n_col = sizes
     dates, rows, cols = obs.shape
@@ -144,20 +147,36 @@
         (has_left, (year, row, col - 1), 4, has_right),
     )
 
+    split = (count + 1) // 2
+    early = (pl.ds(0, split), pl.ds(split, count - split))
+
     def side_copy(step, position, side):
         _, target, slot, _ = sides[side]
+        which = early[side] if side < 2 and step == ITERS else slice(None)
         if side < 2:
             where = pl.ds(chunk_rows(position) + SUB, SUB)
-            landing = year_recv.at[step % 2, side, position]
+            landing = year_recv.at[step % 2, position]
         else:
             group = position // PAIR
             where = pl.ds(pl.multiple_of(wide_start(group) + SUB, SUB), wide_rows)
-            landing = col_recv.at[step % 2, side - 2, group]
+            landing = col_recv.at[step % 2, group]
         return pltpu.make_async_remote_copy(
-            src_ref=field.at[step, 0, :, where, :],
-            dst_ref=field.at[step, slot, :, where, :],
+            src_ref=field.at[step, 0, which, where, :],
+            dst_ref=field.at[step, slot, which, where, :],
             send_sem=send_sem.at[side],
             recv_sem=landing,
+            device_id=target,
+            device_id_type=MESH,
+        )
+
+    def rest_copy(side):
+        _, target, slot, _ = sides[side]
+        which, where = early[1 - side], pl.ds(SUB, rows)
+        return pltpu.make_async_remote_copy(
+            src_ref=field.at[ITERS, 0, which, where, :],
+            dst_ref=field.at[ITERS, slot, which, where, :],
+            send_sem=send_sem.at[side],
+            recv_sem=rest_recv,
             device_id=target,
             device_id_type=MESH,
         )
@@ -202,33 +221,64 @@
             device_id_type=MESH,
         )
 
-    def turn(position, side):
-        return lax.rem(position, 2) == side
-
-    def start_sends(step, position, chosen=range(4), keep=None):
-        for side in chosen:
+    def start_sends(step, position):
+        for side in range(4):
             present = sides[side][0]
             if side >= 2:
                 ready = lax.rem(position, PAIR) == PAIR - 1
                 present = jnp.logical_and(present, ready)
-            elif keep is not None:
-                present = jnp.logical_and(present, keep(position, side))
 
             @pl.when(present)
             def _(side=side):
                 side_copy(step, position, side).start()
 
-    def wait_sides(step, position, chosen=range(4), keep=None):
-        for side in chosen:
-            present = sides[side][3]
-            if side >= 2:
-                present = jnp.logical_and(present, lax.rem(position, PAIR) == 0)
-            elif keep is not None:
-                present = jnp.logical_and(present, keep(position, side))
-
-            @pl.when(present)
-            def _(side=side):
-                side_copy(step, position, side).wait_recv()
+    def wait_pair(first, second, left, right, both):
+        @pl.when(jnp.logical_and(first, second))
+        def _():
+            both.wait_recv()
+
+        @pl.when(jnp.logical_and(first, ~second))
+        def _():
+            left.wait_recv()
+
+        @pl.when(jnp.logical_and(second, ~first))
+        def _():
+            right.wait_recv()
+
+    def landing_of(place, semaphore):
+        return pltpu.make_async_remote_copy(
+            src_ref=place,
+            dst_ref=place,
+            send_sem=send_sem.at[0],
+            recv_sem=semaphore,
+            device_id=sides[0][1],
+            device_id_type=MESH,
+        )
+
+    def wait_years(step, position):
+        where = pl.ds(chunk_rows(position) + SUB, SUB)
+        slots_here = pl.ds(1, 1 if step == ITERS else 2)
+        both = landing_of(
+            field.at[step, slots_here, :, where, :], year_recv.at[step % 2, position]
+        )
+        ends = [side_copy(step, position, side) for side in (0, 1)]
+        wait_pair(has_prev, has_next, *ends, both)
+
+    def wait_cols(step, position):
+        group = position // PAIR
+        where = pl.ds(pl.multiple_of(wide_start(group) + SUB, SUB), wide_rows)
+        both = landing_of(
+            field.at[step, pl.ds(3, 2), :, where, :], col_recv.at[step % 2, group]
+        )
+        ends = [side_copy(step, position, side) for side in (2, 3)]
+
+        @pl.when(lax.rem(position, PAIR) == 0)
+        def _():
+            wait_pair(has_left, has_right, *ends, both)
+
+    def wait_rest():
+        both = landing_of(field.at[ITERS, 1, :, pl.ds(SUB, rows), :], rest_recv)
+        wait_pair(has_prev, has_next, rest_copy(0), rest_copy(1), both)
 
     def close_edges(step, first, last):
         for flag, at_last, present in ((first, False, has_first), (last, True, has_last)):
@@ -397,7 +447,8 @@
         def body(position, carry):
             odd_sum, even_sum = carry
             start, first, last = walk(position)
-            wait_sides(stage, position)
+            wait_cols(stage, position)
+            wait_years(stage, position)
             wait_edges(stage, first, last)
             rows_here = pl.ds(start, SUB)
             held, pushed = [], []
@@ -416,11 +467,19 @@
             for p in range(count):
                 field[stage + 1, 0, p, pl.ds(start + SUB, SUB), :] = turned[p]
             even_sum = even_sum + dot(turned, pushed)
-            start_sends(stage + 1, position, keep=turn if stage + 1 == ITERS else None)
+            start_sends(stage + 1, position)
             close_edges(stage + 1, first, last)
             return odd_sum, even_sum
 
         return body
+
+    def keep_level():
+        if n_col % 2 == 0:
+            partner = col + 1 - 2 * lax.rem(col, 2)
+            pl.semaphore_signal(
+                level_sem, inc=1, device_id=(year, row, partner), device_id_type=MESH
+            )
+            pl.semaphore_wait(level_sem, 1)
 
     for copy in small_loads:
         copy.wait()
@@ -446,6 +505,8 @@
         if stage == 0:
             odd_sum, even_sum = lax.fori_loop(0, chunks + LEAD, opening, (zero, zero))
         else:
+            if stage in LEVEL:
+                keep_level()
             odd_sum, even_sum = lax.fori_loop(0, chunks, make_stage(stage), (zero, zero))
             sums.append(odd_sum)
         sums.append(even_sum)
@@ -484,30 +545,39 @@
     for other in range(1, total_devices):
         sum_copy(0, other).start()
 
-    def send_rest(position, carry):
-        start_sends(ITERS, position, (0, 1), lambda at, side: ~turn(at, side))
-        return carry
-
-    lax.fori_loop(0, chunks, send_rest, 0)
+    for side in range(2):
+        @pl.when(sides[side][0])
+        def _(side=side):
+            rest_copy(side).start()
+
+    def factors(near_side, far_side):
+        return jnp.where(near_side, 2.0, 1.0), jnp.where(far_side, 0.0, 1.0)
+
+    first_edge = [(prev_slot, *factors(has_prev, has_next))] * split
+    first_edge += [(next_slot, *factors(has_next, has_prev))] * (count - split)
+    other_slot = [next_slot] * split + [prev_slot] * (count - split)
 
     def closing(position, last_sum):
         start, first, last = walk(position)
-        later = turn(position, 0)
-        slot = jnp.where(later, prev_slot, next_slot)
-        twice = jnp.where(jnp.where(later, has_prev, has_next), 2.0, 1.0)
-        alone = jnp.where(jnp.where(later, has_next, has_prev), 0.0, 1.0)
-        wait_sides(ITERS, position, keep=turn)
+        rows_here, padded = pl.ds(start, SUB), pl.ds(start + SUB, SUB)
+        wait_cols(ITERS, position)
         wait_edges(ITERS, first, last)
-        held, pushed = [], []
+        held, pushed, planes = [], [], []
         for p in range(count):
             here, plane = plane_sum(ITERS, p, start)
-            beside = field[ITERS, slot, p, pl.ds(start + SUB, SUB), :]
             plane = spatial[p] * plane
-            resid[ITERS, p, pl.ds(start, SUB), :] = plane + temporal[p] * beside
+            planes.append(plane)
             held.append(here)
-            pushed.append(plane + temporal[p] * (twice * beside + alone * here))
+            pushed.append(plane + (temporal[p] * first_edge[p][2]) * here)
         last_sum = last_sum + dot(held, pushed)
-        return last_sum
+        wait_years(ITERS, position)
+        pushed = []
+        for p in range(count):
+            slot, twice, _ = first_edge[p]
+            beside = temporal[p] * field[ITERS, slot, p, padded, :]
+            resid[ITERS, p, rows_here, :] = planes[p] + beside
+            pushed.append(twice * beside)
+        return last_sum + dot(held, pushed)
 
     last_sum = lax.fori_loop(0, chunks, closing, zero)
     notes[1, 0:1, :] = jnp.sum(last_sum, axis=0, keepdims=True)
@@ -571,31 +641,30 @@
 
     def prepare(position, carry):
         start, _, _ = walk(position)
-        slot = jnp.where(turn(position, 0), next_slot, prev_slot)
-        wait_sides(ITERS, position, (0, 1), lambda at, side: ~turn(at, side))
         rows_here, padded = pl.ds(start, SUB), pl.ds(start + SUB, SUB)
         for p in range(count):
             vectors = [field[j + 1, 0, p, padded, :] for j in range(ITERS)]
             total = field[0, 0, p, padded, :]
             for pace, vector in zip(paces, vectors):
                 total = total + pace * vector
-            new_params[0, p, rows_here, :] = total
+            anchor[0, p, rows_here, :] = total
             total = steers[0] * vectors[0]
             for steer, vector in zip(steers[1:], vectors[1:]):
                 total = total + steer * vector
             slope[0, p, rows_here, :] = total
             vectors = [resid[j, p, rows_here, :] for j in range(ITERS + 1)]
-            vectors[-1] = vectors[-1] + temporal[p] * field[ITERS, slot, p, padded, :]
+            vectors[-1] = vectors[-1] + temporal[p] * field[ITERS, other_slot[p], p, padded, :]
             total = base_mix[0] * vectors[0]
             for mix, vector in zip(base_mix[1:], vectors[1:]):
                 total = total + mix * vector
-            residual[0, p, rows_here, :] = total
+            anchor[1, p, rows_here, :] = total
             total = slope_mix[0] * vectors[0]
             for mix, vector in zip(slope_mix[1:], vectors[1:]):
                 total = total + mix * vector
             slope[1, p, rows_here, :] = total
         return carry
 
+    wait_rest()
     lax.fori_loop(0, chunks, prepare, 0)
 
     for side in range(4):
@@ -611,31 +680,26 @@
     sum_copies(0).wait_send()
 
     final = jnp.broadcast_to(jnp.sum(gather(1), axis=1, keepdims=True), (1, cols))
-    alpha = jnp.broadcast_to(inner / (curve - bend * final), (SUB, cols))
-
-    def finish(b, carry):
-        rows_here = pl.ds(pl.multiple_of(b * SUB, SUB), SUB)
-        for p in range(count):
-            new_params[0, p, rows_here, :] = (
-                new_params[0, p, rows_here, :] + alpha * slope[0, p, rows_here, :]
+    pace[...] = jnp.broadcast_to(inner / (curve - bend * final), (SUB, cols))
+
+    sum_copies(1).wait_send()
+
+
+def store_kernel(anchor, slope, pace, new_params, residual, total, sem):
+    count = total.shape[1]
+    step = jnp.broadcast_to(pace[0:1, :], total.shape[1:])
+    half = (count + 1) // 2
+    copies = []
+    for at, out in enumerate((new_params, residual)):
+        for piece, (low, high) in enumerate(((0, half), (half, count))):
+            where = pl.ds(low, high - low)
+            total[at, where] = anchor[at, where] + step[low:high] * slope[at, where]
+            copies.append(
+                pltpu.make_async_copy(
+                    total.at[at, where], out.at[0, where], sem.at[at, piece]
+                )
             )
-            residual[0, p, rows_here, :] = (
-                residual[0, p, rows_here, :] + alpha * slope[1, p, rows_here, :]
-            )
-        return carry
-
-    lax.fori_loop(0, rows // SUB, finish, 0)
-
-    sum_copies(1).wait_send()
-
-
-def store_kernel(new_params, residual, new_params_out, residual_out, sem):
-    copies = (
-        pltpu.make_async_copy(new_params, new_params_out, sem.at[0]),
-        pltpu.make_async_copy(residual, residual_out, sem.at[1]),
-    )
-    for copy in copies:
-        copy.start()
+            copies[-1].start()
     for copy in copies:
         copy.wait()
 
@@ -651,12 +715,12 @@
     vmem = pl.BlockSpec(memory_space=pltpu.VMEM)
     hbm = pl.BlockSpec(memory_space=pltpu.HBM)
     dma = pltpu.SemaphoreType.DMA
-    outs = (jax.ShapeDtypeStruct(params.shape, f32), jax.ShapeDtypeStruct(params.shape, f32))
+    both = jax.ShapeDtypeStruct((2, count, rows, cols), f32)
     results = pl.pallas_call(
         functools.partial(kernel, sizes),
-        out_shape=outs,
+        out_shape=(both, both, jax.ShapeDtypeStruct((SUB, cols), f32)),
         in_specs=[hbm] * 6,
-        out_specs=(vmem, vmem),
+        out_specs=(vmem, vmem, vmem),
         scratch_shapes=[
             pltpu.VMEM((dates, rows, cols), f32),
             pltpu.VMEM((dates, rows, cols), jnp.int32),
@@ -666,18 +730,19 @@
             pltpu.VMEM((ROUNDS, 5, count, rows + 2 * SUB, cols), f32),
             pltpu.VMEM((count * (count + 1) // 2, rows, cols), f32),
             pltpu.VMEM((ROUNDS, count, rows, cols), f32),
-            pltpu.VMEM((2, count, rows, cols), f32),
             pltpu.VMEM((SUB, cols), f32),
             pltpu.VMEM((2, SUB, cols), f32),
             pltpu.VMEM((2, max(others, 1), cols), f32),
             dma((4 + 2 * groups,)),
             dma((4,)),
-            dma((2, 2, chunks)),
-            dma((2, 2, groups)),
+            dma((2, chunks)),
+            dma((2, groups)),
+            dma(()),
             dma((2,)),
             dma((2, 2)),
             dma((2,)),
             dma((2,)),
+            pltpu.SemaphoreType.REGULAR,
         ],
         compiler_params=pltpu.CompilerParams(
             collective_id=0, has_side_effects=True, vmem_limit_bytes=24 * 2**20
@@ -693,11 +758,14 @@
     )
     return pl.pallas_call(
         store_kernel,
-        out_shape=outs,
-        in_specs=[vmem, vmem],
+        out_shape=(
+            jax.ShapeDtypeStruct(params.shape, f32),
+            jax.ShapeDtypeStruct(params.shape, f32),
+        ),
+        in_specs=[vmem, vmem, vmem],
         out_specs=(hbm, hbm),
-        scratch_shapes=[dma((2,))],
-        compiler_params=pltpu.CompilerParams(vmem_limit_bytes=2**20),
+        scratch_shapes=[pltpu.VMEM((2, count, rows, cols), f32), dma((2, 2))],
+        compiler_params=pltpu.CompilerParams(vmem_limit_bytes=4 * 2**20),
         name="store",
     )(*results)
 

time: 37.1 us -> 36.6 us (0.987)
  Pallas kernels: 36.3 us -> 35.8 us
    pallas_call x2, Pallas kernels: 36.3 us -> 35.8 us  [the longest x1 35 us: per_device(): pl.pallas_call(functools.partial(kernel, sizes), out_shape=(both, both, j...]
where the time goes in v3:
time: 36.6 us; the launch traced here: 36.4 us
  Pallas kernels  35.8 us (98%)
  between operations  0.64 us (2%)
    pallas_call x1, Pallas kernels, per_device(): pl.pallas_call(functools.partial(kernel, sizes), out_shape=(both, both, j...  35 us
    pallas_call x1, Pallas kernels, per_device(): pl.pallas_call(store_kernel, out_shape=(jax.ShapeDtypeStruct(params.shape...  0.81 us

profile of v3, /device:TPU:0, one launch (start us, length us, event | category | flops | bytes accessed | tf_op | source)
XLA Modules:
  0.0 36.4 jit_solution(7847536853734324395)
XLA Ops:
  0.6 35.0 %gauss_newton.1 = (f32[2,7,64,128]{3,2,1,0:T(8,128)S(1)}, f32[2,7,64,128]{3,2,1,0:T(8,128)S(1)}, f32[8,128]{1,0:T(8,128)S(1)}) custom-call(f32[1,46,64,128]{3,2,1,0:T(8,128)} %observed.1, s32[1,46,64,128]{3,2,1,0:T(8,128)} %quality.1, s32[64,128]{1,0:T(8,128)} %land_mask.1, f32[1,7,64,128]{3,2,1,0:T(8,128)} %params.1, f32[7]{0:T(128)} %spatial_weight.1, ...), custom_call_target="tpu_custom_call" | custom-call | tf_op jit(solution)/shard_map/gauss_newton/pallas_call | solution.py:719
  35.6 0.8 %store.1 = (f32[1,7,64,128]{3,2,1,0:T(8,128)}, f32[1,7,64,128]{3,2,1,0:T(8,128)}) custom-call(f32[2,7,64,128]{3,2,1,0:T(8,128)S(1)} %get-tuple-element.5.anchor, f32[2,7,64,128]{3,2,1,0:T(8,128)S(1)} %get-tuple-element.6.slope, f32[8,128]{1,0:T(8,128)S(1)} %get-tuple-element.7.pace), custom_call_target="tpu_custom_call" | custom-call | tf_op jit(solution)/shard_map/store/pallas_call | solution.py:759

commit v4 on v3

--- a/solution.py
+++ b/solution.py
@@ -21,7 +21,7 @@
     return [(i, j) for i in range(count) for j in range(i, count)]
 
 
-def kernel(
+def solve(
     sizes,
     observed,
     quality,
@@ -53,6 +53,8 @@
     sum_send,
     sum_recv,
     level_sem,
+    last_send,
+    last_recv,
 ):
     n_year, n_row, n_col = sizes
     dates, rows, cols = obs.shape
@@ -513,29 +515,17 @@
 
     others = total_devices - 1
 
+    note_sems = ((sum_send, sum_recv), (last_send, last_recv))
+
     def sum_copy(note, other):
         return pltpu.make_async_remote_copy(
             src_ref=notes.at[note, pl.ds(0, 1)],
             dst_ref=slots.at[note, pl.ds(other - 1, 1)],
-            send_sem=sum_send.at[note],
-            recv_sem=sum_recv.at[note],
+            send_sem=note_sems[note][0],
+            recv_sem=note_sems[note][1],
             device_id=peer(other),
             device_id_type=MESH,
         )
-
-    def sum_copies(note):
-        return pltpu.make_async_remote_copy(
-            src_ref=slots.at[note],
-            dst_ref=slots.at[note],
-            send_sem=sum_send.at[note],
-            recv_sem=sum_recv.at[note],
-            device_id=peer(1),
-            device_id_type=MESH,
-        )
-
-    def gather(note):
-        sum_copies(note).wait_recv()
-        return jnp.sum(slots[note], axis=0, keepdims=True) + notes[note, 0:1, :]
 
     for at, value in enumerate(sums):
         moments[at : at + 1, :] = jnp.sum(value, axis=0, keepdims=True)
@@ -584,7 +574,8 @@
     for other in range(1, total_devices):
         sum_copy(1, other).start()
 
-    known = jnp.where(lane == level, jnp.broadcast_to(gather(0), (SUB, cols)), 0.0)
+    known = gather(slots, notes, 0, *note_sems[0], peer(1))
+    known = jnp.where(lane == level, jnp.broadcast_to(known, (SUB, cols)), 0.0)
     known = jnp.broadcast_to(jnp.sum(known, axis=1, keepdims=True), (SUB, cols))
     mu = [known[at : at + 1, :] for at in range(2 * ITERS - 1)]
     drop = [mu[at] - mu[at + 1] for at in range(2 * ITERS - 2)]
@@ -677,12 +668,57 @@
         def _(at_last=at_last):
             row_sends(at_last).wait_send()
 
-    sum_copies(0).wait_send()
-
-    final = jnp.broadcast_to(jnp.sum(gather(1), axis=1, keepdims=True), (1, cols))
-    pace[...] = jnp.broadcast_to(inner / (curve - bend * final), (SUB, cols))
-
-    sum_copies(1).wait_send()
+    note_copies(slots, 0, *note_sems[0], peer(1)).wait_send()
+
+    return inner, curve, bend
+
+
+def note_copies(slots, note, send, recv, device):
+    return pltpu.make_async_remote_copy(
+        src_ref=slots.at[note],
+        dst_ref=slots.at[note],
+        send_sem=send,
+        recv_sem=recv,
+        device_id=device,
+        device_id_type=MESH,
+    )
+
+
+def gather(slots, notes, note, send, recv, device):
+    note_copies(slots, note, send, recv, device).wait_recv()
+    return jnp.sum(slots[note], axis=0, keepdims=True) + notes[note, 0:1, :]
+
+
+def kernel(sizes, *refs):
+    *refs, last_send, last_recv = refs
+    pace, notes, slots = refs[8], refs[-2], refs[-1]
+    obs = refs[9]
+    chunks = obs.shape[1] // SUB
+    groups = chunks // PAIR
+    dma = pltpu.SemaphoreType.DMA
+
+    def scope(*sems):
+        return solve(sizes, *refs, *sems, last_send, last_recv)
+
+    inner, curve, bend = pl.run_scoped(
+        scope,
+        dma((4 + 2 * groups,)),
+        dma((4,)),
+        dma((2, chunks)),
+        dma((2, groups)),
+        dma(()),
+        dma((2,)),
+        dma((2, 2)),
+        dma(()),
+        dma(()),
+        pltpu.SemaphoreType.REGULAR,
+    )
+    years, rows, cols = (lax.axis_index(axis) for axis in ("year", "row", "col"))
+    device = (years, rows, lax.rem(cols + 1, sizes[2]))
+    final = gather(slots, notes, 1, last_send, last_recv, device)
+    final = jnp.broadcast_to(jnp.sum(final, axis=1, keepdims=True), final.shape)
+    pace[...] = jnp.broadcast_to(inner / (curve - bend * final), pace.shape)
+    note_copies(slots, 1, last_send, last_recv, device).wait_send()
 
 
 def store_kernel(anchor, slope, pace, new_params, residual, total, sem):
@@ -733,16 +769,8 @@
             pltpu.VMEM((SUB, cols), f32),
             pltpu.VMEM((2, SUB, cols), f32),
             pltpu.VMEM((2, max(others, 1), cols), f32),
-            dma((4 + 2 * groups,)),
-            dma((4,)),
-            dma((2, chunks)),
-            dma((2, groups)),
             dma(()),
-            dma((2,)),
-            dma((2, 2)),
-            dma((2,)),
-            dma((2,)),
-            pltpu.SemaphoreType.REGULAR,
+            dma(()),
         ],
         compiler_params=pltpu.CompilerParams(
             collective_id=0, has_side_effects=True, vmem_limit_bytes=24 * 2**20

time: 36.6 us -> 36.1 us (0.986)
  Pallas kernels: 35.8 us -> 35.4 us
    pallas_call x1, Pallas kernels: 35 us -> 34.5 us  [per_device(): pl.pallas_call(functools.partial(kernel, sizes), out_shape=(both, both, j...]
where the time goes in v4:
time: 36.1 us; the launch traced here: 36 us
  Pallas kernels  35.4 us (98%)
  between operations  0.64 us (2%)
    pallas_call x1, Pallas kernels, per_device(): pl.pallas_call(functools.partial(kernel, sizes), out_shape=(both, both, j...  34.5 us
    pallas_call x1, Pallas kernels, per_device(): pl.pallas_call(store_kernel, out_shape=(jax.ShapeDtypeStruct(params.shape...  0.81 us

profile of v4, /device:TPU:0, one launch (start us, length us, event | category | flops | bytes accessed | tf_op | source)
XLA Modules:
  0.0 36.0 jit_solution(7326679183659927288)
XLA Ops:
  0.6 34.5 %gauss_newton.1 = (f32[2,7,64,128]{3,2,1,0:T(8,128)S(1)}, f32[2,7,64,128]{3,2,1,0:T(8,128)S(1)}, f32[8,128]{1,0:T(8,128)S(1)}) custom-call(f32[1,46,64,128]{3,2,1,0:T(8,128)} %refs_0_.1, s32[1,46,64,128]{3,2,1,0:T(8,128)} %refs_1_.1, s32[64,128]{1,0:T(8,128)} %refs_2_.1, f32[1,7,64,128]{3,2,1,0:T(8,128)} %refs_3_.1, f32[7]{0:T(128)} %refs_4_.1, f32[7]{0:T(128)} %refs_5_.1), custom_call_target="tpu_custom_call" | custom-call | tf_op jit(solution)/shard_map/gauss_newton/pallas_call | solution.py:755
  35.2 0.8 %store.1 = (f32[1,7,64,128]{3,2,1,0:T(8,128)}, f32[1,7,64,128]{3,2,1,0:T(8,128)}) custom-call(f32[2,7,64,128]{3,2,1,0:T(8,128)S(1)} %get-tuple-element.5.anchor, f32[2,7,64,128]{3,2,1,0:T(8,128)S(1)} %get-tuple-element.6.slope, f32[8,128]{1,0:T(8,128)S(1)} %get-tuple-element.7.pace), custom_call_target="tpu_custom_call" | custom-call | tf_op jit(solution)/shard_map/store/pallas_call | solution.py:787

commit v5 on v4

--- a/solution.py
+++ b/solution.py
@@ -149,7 +149,7 @@
         (has_left, (year, row, col - 1), 4, has_right),
     )
 
-    split = (count + 1) // 2
+    split = count // 2
     early = (pl.ds(0, split), pl.ds(split, count - split))
 
     def side_copy(step, position, side):
@@ -171,9 +171,9 @@
             device_id_type=MESH,
         )
 
-    def rest_copy(side):
+    def rest_copy(side, low=0, high=rows):
         _, target, slot, _ = sides[side]
-        which, where = early[1 - side], pl.ds(SUB, rows)
+        which, where = early[1 - side], pl.ds(SUB + low, high - low)
         return pltpu.make_async_remote_copy(
             src_ref=field.at[ITERS, 0, which, where, :],
             dst_ref=field.at[ITERS, slot, which, where, :],
@@ -527,6 +527,15 @@
             device_id_type=MESH,
         )
 
+    def start_rest(low, high):
+        for side in range(2):
+            @pl.when(sides[side][0])
+            def _(side=side):
+                rest_copy(side, low, high).start()
+
+    cut, tail = rows // 2 // SUB * SUB, rows // 4 // SUB * SUB
+    start_rest(0, cut)
+
     for at, value in enumerate(sums):
         moments[at : at + 1, :] = jnp.sum(value, axis=0, keepdims=True)
     moments[len(sums) : SUB, :] = jnp.zeros((SUB - len(sums), cols), jnp.float32)
@@ -535,10 +544,7 @@
     for other in range(1, total_devices):
         sum_copy(0, other).start()
 
-    for side in range(2):
-        @pl.when(sides[side][0])
-        def _(side=side):
-            rest_copy(side).start()
+    start_rest(cut, rows - tail)
 
     def factors(near_side, far_side):
         return jnp.where(near_side, 2.0, 1.0), jnp.where(far_side, 0.0, 1.0)
@@ -573,6 +579,7 @@
     notes[1, 0:1, :] = jnp.sum(last_sum, axis=0, keepdims=True)
     for other in range(1, total_devices):
         sum_copy(1, other).start()
+    start_rest(rows - tail, rows)
 
     known = gather(slots, notes, 0, *note_sems[0], peer(1))
     known = jnp.where(lane == level, jnp.broadcast_to(known, (SUB, cols)), 0.0)

time: 36.1 us -> 35.9 us (level)
  no operation moved by 1% of the time
where the time goes in v5:
time: 35.9 us; the launch traced here: 35.8 us
  Pallas kernels  35.2 us (98%)
  between operations  0.64 us (2%)
    pallas_call x1, Pallas kernels, per_device(): pl.pallas_call(functools.partial(kernel, sizes), out_shape=(both, both, j...  34.3 us
    pallas_call x1, Pallas kernels, per_device(): pl.pallas_call(store_kernel, out_shape=(jax.ShapeDtypeStruct(params.shape...  0.81 us

profile of v5, /device:TPU:0, one launch (start us, length us, event | category | flops | bytes accessed | tf_op | source)
XLA Modules:
  0.0 35.8 jit_solution(9788907649277321609)
XLA Ops:
  0.6 34.3 %gauss_newton.1 = (f32[2,7,64,128]{3,2,1,0:T(8,128)S(1)}, f32[2,7,64,128]{3,2,1,0:T(8,128)S(1)}, f32[8,128]{1,0:T(8,128)S(1)}) custom-call(f32[1,46,64,128]{3,2,1,0:T(8,128)} %refs_0_.1, s32[1,46,64,128]{3,2,1,0:T(8,128)} %refs_1_.1, s32[64,128]{1,0:T(8,128)} %refs_2_.1, f32[1,7,64,128]{3,2,1,0:T(8,128)} %refs_3_.1, f32[7]{0:T(128)} %refs_4_.1, f32[7]{0:T(128)} %refs_5_.1), custom_call_target="tpu_custom_call" | custom-call | tf_op jit(solution)/shard_map/gauss_newton/pallas_call | solution.py:762
  35.0 0.8 %store.1 = (f32[1,7,64,128]{3,2,1,0:T(8,128)}, f32[1,7,64,128]{3,2,1,0:T(8,128)}) custom-call(f32[2,7,64,128]{3,2,1,0:T(8,128)S(1)} %get-tuple-element.5.anchor, f32[2,7,64,128]{3,2,1,0:T(8,128)S(1)} %get-tuple-element.6.slope, f32[8,128]{1,0:T(8,128)S(1)} %get-tuple-element.7.pace), custom_call_target="tpu_custom_call" | custom-call | tf_op jit(solution)/shard_map/store/pallas_call | solution.py:794

commit v6 on v5

--- a/solution.py
+++ b/solution.py
@@ -12,7 +12,7 @@
 SUB = 8
 LEAD = 2
 PAIR = 2
-LEVEL = (1, 2, 3)
+LEVEL = (1, 3)
 DAMPING = 0.1
 MESH = pl.DeviceIdType.MESH
 
@@ -533,7 +533,7 @@
             def _(side=side):
                 rest_copy(side, low, high).start()
 
-    cut, tail = rows // 2 // SUB * SUB, rows // 4 // SUB * SUB
+    cut, tail = rows // 2 // SUB * SUB, 3 * rows // 8 // SUB * SUB
     start_rest(0, cut)
 
     for at, value in enumerate(sums):

time: 35.9 us -> 35.9 us (level)
  no operation moved by 1% of the time
where the time goes in v6:
time: 35.9 us; the launch traced here: 35.7 us
  Pallas kernels  35.1 us (98%)
  between operations  0.64 us (2%)
    pallas_call x1, Pallas kernels, per_device(): pl.pallas_call(functools.partial(kernel, sizes), out_shape=(both, both, j...  34.3 us
    pallas_call x1, Pallas kernels, per_device(): pl.pallas_call(store_kernel, out_shape=(jax.ShapeDtypeStruct(params.shape...  0.81 us

profile of v6, /device:TPU:0, one launch (start us, length us, event | category | flops | bytes accessed | tf_op | source)
XLA Modules:
  0.0 35.7 jit_solution(1141686412198796847)
XLA Ops:
  0.6 34.3 %gauss_newton.1 = (f32[2,7,64,128]{3,2,1,0:T(8,128)S(1)}, f32[2,7,64,128]{3,2,1,0:T(8,128)S(1)}, f32[8,128]{1,0:T(8,128)S(1)}) custom-call(f32[1,46,64,128]{3,2,1,0:T(8,128)} %refs_0_.1, s32[1,46,64,128]{3,2,1,0:T(8,128)} %refs_1_.1, s32[64,128]{1,0:T(8,128)} %refs_2_.1, f32[1,7,64,128]{3,2,1,0:T(8,128)} %refs_3_.1, f32[7]{0:T(128)} %refs_4_.1, f32[7]{0:T(128)} %refs_5_.1), custom_call_target="tpu_custom_call" | custom-call | tf_op jit(solution)/shard_map/gauss_newton/pallas_call | solution.py:762
  34.9 0.8 %store.1 = (f32[1,7,64,128]{3,2,1,0:T(8,128)}, f32[1,7,64,128]{3,2,1,0:T(8,128)}) custom-call(f32[2,7,64,128]{3,2,1,0:T(8,128)S(1)} %get-tuple-element.5.anchor, f32[2,7,64,128]{3,2,1,0:T(8,128)S(1)} %get-tuple-element.6.slope, f32[8,128]{1,0:T(8,128)S(1)} %get-tuple-element.7.pace), custom_call_target="tpu_custom_call" | custom-call | tf_op jit(solution)/shard_map/store/pallas_call | solution.py:794

commit v7 on v6

--- a/solution.py
+++ b/solution.py
@@ -517,13 +517,18 @@
 
     note_sems = ((sum_send, sum_recv), (last_send, last_recv))
 
-    def sum_copy(note, other):
+    me = (year * n_row + row) * n_col + col
+
+    def sum_copy(note, turn):
+        below = (turn < me).astype(jnp.int32)
+        target = turn + 1 - below
+        landing = me - below
         return pltpu.make_async_remote_copy(
             src_ref=notes.at[note, pl.ds(0, 1)],
-            dst_ref=slots.at[note, pl.ds(other - 1, 1)],
+            dst_ref=slots.at[note, pl.ds(landing, 1)],
             send_sem=note_sems[note][0],
             recv_sem=note_sems[note][1],
-            device_id=peer(other),
+            device_id=peer(target - me + total_devices),
             device_id_type=MESH,
         )
 
@@ -541,8 +546,8 @@
     moments[len(sums) : SUB, :] = jnp.zeros((SUB - len(sums), cols), jnp.float32)
     folded = jnp.broadcast_to(jnp.sum(moments[...], axis=1, keepdims=True), (SUB, cols))
     notes[0, 0:1, :] = jnp.sum(jnp.where(lane == level, folded, 0.0), axis=0, keepdims=True)
-    for other in range(1, total_devices):
-        sum_copy(0, other).start()
+    for turn in range(total_devices - 1):
+        sum_copy(0, turn).start()
 
     start_rest(cut, rows - tail)
 
@@ -577,8 +582,8 @@
 
     last_sum = lax.fori_loop(0, chunks, closing, zero)
     notes[1, 0:1, :] = jnp.sum(last_sum, axis=0, keepdims=True)
-    for other in range(1, total_devices):
-        sum_copy(1, other).start()
+    for turn in range(total_devices - 1):
+        sum_copy(1, turn).start()
     start_rest(rows - tail, rows)
 
     known = gather(slots, notes, 0, *note_sems[0], peer(1))

time: 35.9 us -> 35.9 us (level)
  no operation moved by 1% of the time
where the time goes in v7:
time: 35.9 us; the launch traced here: 35.7 us
  Pallas kernels  35.1 us (98%)
  between operations  0.64 us (2%)
    pallas_call x1, Pallas kernels, per_device(): pl.pallas_call(functools.partial(kernel, sizes), out_shape=(both, both, j...  34.3 us
    pallas_call x1, Pallas kernels, per_device(): pl.pallas_call(store_kernel, out_shape=(jax.ShapeDtypeStruct(params.shape...  0.81 us

profile of v7, /device:TPU:0, one launch (start us, length us, event | category | flops | bytes accessed | tf_op | source)
XLA Modules:
  0.0 35.7 jit_solution(10321028288993624317)
XLA Ops:
  0.6 34.3 %gauss_newton.1 = (f32[2,7,64,128]{3,2,1,0:T(8,128)S(1)}, f32[2,7,64,128]{3,2,1,0:T(8,128)S(1)}, f32[8,128]{1,0:T(8,128)S(1)}) custom-call(f32[1,46,64,128]{3,2,1,0:T(8,128)} %refs_0_.1, s32[1,46,64,128]{3,2,1,0:T(8,128)} %refs_1_.1, s32[64,128]{1,0:T(8,128)} %refs_2_.1, f32[1,7,64,128]{3,2,1,0:T(8,128)} %refs_3_.1, f32[7]{0:T(128)} %refs_4_.1, f32[7]{0:T(128)} %refs_5_.1), custom_call_target="tpu_custom_call" | custom-call | tf_op jit(solution)/shard_map/gauss_newton/pallas_call | solution.py:767
  34.9 0.8 %store.1 = (f32[1,7,64,128]{3,2,1,0:T(8,128)}, f32[1,7,64,128]{3,2,1,0:T(8,128)}) custom-call(f32[2,7,64,128]{3,2,1,0:T(8,128)S(1)} %get-tuple-element.5.anchor, f32[2,7,64,128]{3,2,1,0:T(8,128)S(1)} %get-tuple-element.6.slope, f32[8,128]{1,0:T(8,128)S(1)} %get-tuple-element.7.pace), custom_call_target="tpu_custom_call" | custom-call | tf_op jit(solution)/shard_map/store/pallas_call | solution.py:799
